TPU v7x, 32 devices: a whole 2x2x4 slice. The times are simulated.
32 devices in a mesh: rows: 8 (over z, y), batch: 4 (over x, core).
Axes of the slice: x: 2, y: 2, z: 4, core: 2. Of those that a mesh axis runs over, the one named last changes fastest.
Arguments:
- patches: bfloat16 [16, 56, 56, 384], P('batch', 'rows'), may hold values from -6 to 6
- widths: int32 [16], P('batch'), may hold values from 29 to 56, as said below
- keep_mask: int32 [16, 2], P('batch'), may hold values 0 or 1
- pre_gain: bfloat16 [384], replicated, may hold values from 0.5 to 1.5
- pre_shift: bfloat16 [384], replicated, may hold values from -3 to 3
- in_weight: bfloat16 [384, 1152], replicated, may hold values from -0.3125 to 0.3125
- in_bias: bfloat16 [768], replicated, may hold values from -3 to 3
- bias_table: bfloat16 [169, 12], replicated, may hold values from -4 to 4
- out_weight: bfloat16 [384, 384], replicated, may hold values from -1.25 to 1.25
- out_bias: bfloat16 [384], replicated, may hold values from -3 to 3
- mid_gain: bfloat16 [384], replicated, may hold values from 0.5 to 1.5
- mid_shift: bfloat16 [384], replicated, may hold values from -3 to 3
- up_weight: bfloat16 [384, 1536], replicated, may hold values from -0.3125 to 0.3125
- up_bias: bfloat16 [1536], replicated, may hold values from -3 to 3
- down_weight: bfloat16 [1536, 384], replicated, may hold values from -0.15625 to 0.15625
- down_bias: bfloat16 [384], replicated, may hold values from -3 to 3
- cotangent: bfloat16 [16, 56, 56, 384], P('batch', 'rows'), may hold values from -6 to 6
Outputs:
- output: bfloat16 [16, 56, 56, 384], P('batch', 'rows')
- grad_patches: float32 [16, 56, 56, 384], P('batch', 'rows')
- grad_pre_gain: float32 [384], replicated
- grad_pre_shift: float32 [384], replicated
- grad_in_weight: float32 [384, 1152], replicated
- grad_in_bias: float32 [768], replicated
- grad_bias_table: float32 [169, 12], replicated
- grad_out_weight: float32 [384, 384], replicated
- grad_out_bias: float32 [384], replicated
- grad_mid_gain: float32 [384], replicated
- grad_mid_shift: float32 [384], replicated
- grad_up_weight: float32 [384, 1536], replicated
- grad_up_bias: float32 [1536], replicated
- grad_down_weight: float32 [1536, 384], replicated
- grad_down_bias: float32 [384], replicated
Inputs may be any that keep to these rules, and one draw needn't show every extreme that they name: `widths`: every draw holds an image of the full canvas width 56 and one of width 56 // 2 + 1.
All inputs are finite; a program needn't handle non-finite values. No bound on the sum of `keep_mask` on one device may be relied on, other than what follows from the above.
Results may differ from a plain program's by a relative error of at most 0.012.
Values may be sent and summed in bfloat16 or wider, within the bound.
No kernel may reach another device: no remote copies, remote signals or barrier semaphores. Data moves between devices by JAX's collectives and lax.ppermute only.
A program may use at most 192 MiB of HBM per device.

v0:
```python
import math

import jax
import jax.numpy as jnp
from jax import lax
from jax.sharding import PartitionSpec as P

HEADS = 12
WIN = 7
SHIFT = 3


EPSILON = 1e-05
KEEP_RATE = 0.8
MASKED = -100.0


def passed_along(array, axis, by):
    count = lax.axis_size(axis)
    return lax.ppermute(array, axis, [(i, (i + by) % count) for i in range(count)])


def layer_norm(values, gain, shift):
    centred = values - jnp.mean(values, axis=-1, keepdims=True)
    spread = jnp.mean(centred * centred, axis=-1, keepdims=True)
    return centred * lax.rsqrt(spread + EPSILON) * gain + shift


def gelu_exact(values):
    return jax.nn.gelu(values, approximate=False)


def to_windows(canvas):
    images, height, columns, channels = canvas.shape
    blocked = canvas.reshape(images, height // WIN, WIN, columns // WIN, WIN, channels)
    return blocked.transpose(0, 1, 3, 2, 4, 5).reshape(-1, WIN * WIN, channels)


def from_windows(blocked, images, height, columns):
    channels = blocked.shape[-1]
    canvas = blocked.reshape(images, height // WIN, columns // WIN, WIN, WIN, channels)
    return canvas.transpose(0, 1, 3, 2, 4, 5).reshape(images, height, columns, channels)


def table_onehot():
    places = jnp.arange(WIN * WIN, dtype=jnp.int32)
    row_pos = places // WIN
    col_pos = places % WIN
    table_index = (row_pos[:, None] - row_pos[None, :] + WIN - 1) * (2 * WIN - 1) + (
        col_pos[:, None] - col_pos[None, :] + WIN - 1
    )
    entries = jnp.arange((2 * WIN - 1) ** 2, dtype=jnp.int32)
    return table_index.reshape(-1)[:, None] == entries[None, :]


def region_ids(row_glob, total_rows, columns):
    row_region = (row_glob >= total_rows - WIN).astype(jnp.int32) + (
        row_glob >= total_rows - SHIFT
    ).astype(jnp.int32)
    col_glob = jnp.arange(columns, dtype=jnp.int32)
    col_region = (col_glob >= columns - WIN).astype(jnp.int32) + (
        col_glob >= columns - SHIFT
    ).astype(jnp.int32)
    return row_region[:, None] * 3 + col_region[None, :]


def on_device(
    patches,
    widths,
    keep_mask,
    pre_gain,
    pre_shift,
    in_weight,
    in_bias,
    bias_table,
    out_weight,
    out_bias,
    mid_gain,
    mid_shift,
    up_weight,
    up_bias,
    down_weight,
    down_bias,
    cotangent,
):
    single = jnp.float32
    half = jnp.bfloat16
    images, height, columns, channels = patches.shape
    head_size = channels // HEADS
    factor = 1.0 / math.sqrt(head_size)
    halo_rows = passed_along(patches[:, :SHIFT], "rows", -1)
    extended = jnp.concatenate([patches[:, SHIFT:], halo_rows], axis=1)
    shifted = jnp.roll(extended, -SHIFT, axis=2)
    tokens = to_windows(shifted).reshape(-1, channels)
    window_count = tokens.shape[0] // (WIN * WIN)
    col_glob = jnp.arange(columns, dtype=jnp.int32)
    valid_cols = (((col_glob + SHIFT) % columns)[None, :] < widths[:, None]).astype(single)
    valid_grid = jnp.broadcast_to(valid_cols[:, None, :, None], (images, height, columns, 1))
    keep_rates = keep_mask.astype(single) / KEEP_RATE
    valid_tok = to_windows(valid_grid).reshape(-1, 1)
    attn_scale = to_windows(valid_grid * keep_rates[:, 0][:, None, None, None]).reshape(-1, 1)
    mlp_scale = to_windows(valid_grid * keep_rates[:, 1][:, None, None, None]).reshape(-1, 1)
    row_glob = lax.axis_index("rows") * height + jnp.arange(height, dtype=jnp.int32)
    regions = region_ids(row_glob, height * lax.axis_size("rows"), columns)
    region_win = to_windows(
        jnp.broadcast_to(regions[None, :, :, None], (images, height, columns, 1))
    )[:, :, 0]
    shift_add = jnp.where(region_win[:, :, None] == region_win[:, None, :], 0.0, MASKED).astype(
        single
    )
    onehot = table_onehot()
    pair_bias = jnp.dot(onehot.astype(half), bias_table, preferred_element_type=single)
    pair_bias = pair_bias.T.reshape(HEADS, WIN * WIN, WIN * WIN)
    score_add = pair_bias[None] + shift_add[:, None]

    def attention_scores(query_part, key_part):
        raw_scores = jnp.einsum(
            "wqhd,wkhd->whqk", query_part, key_part, preferred_element_type=single
        )
        return raw_scores * factor + score_add

    inputs = tokens.astype(single)
    norm_one, norm_one_back = jax.vjp(
        layer_norm, inputs, pre_gain.astype(single), pre_shift.astype(single)
    )
    hidden_one = (norm_one * valid_tok).astype(half)
    bias_full = jnp.concatenate(
        [
            in_bias[:channels].astype(single),
            jnp.zeros((channels,), single),
            in_bias[channels:].astype(single),
        ]
    )
    projected = jnp.dot(hidden_one, in_weight, preferred_element_type=single) + bias_full
    heads_shape = (window_count, WIN * WIN, HEADS, head_size)
    queries = projected[:, :channels].astype(half).reshape(heads_shape)
    keys_all = projected[:, channels : 2 * channels].astype(half).reshape(heads_shape)
    vals_all = projected[:, 2 * channels :].astype(half).reshape(heads_shape)
    scores = attention_scores(queries, keys_all)
    log_total = jax.nn.logsumexp(scores, axis=-1, keepdims=True)
    probs_low = jnp.exp(scores - log_total).astype(half)
    mixed = (
        jnp.einsum("whqk,wkhd->wqhd", probs_low, vals_all, preferred_element_type=single)
        .reshape(-1, channels)
        .astype(half)
    )
    attn_out = jnp.dot(mixed, out_weight, preferred_element_type=single) + out_bias.astype(single)
    after_attn = inputs + attn_scale * attn_out
    norm_two, norm_two_back = jax.vjp(
        layer_norm, after_attn, mid_gain.astype(single), mid_shift.astype(single)
    )
    hidden_two = norm_two.astype(half)
    pre_act = jnp.dot(hidden_two, up_weight, preferred_element_type=single) + up_bias.astype(single)
    activated, act_back = jax.vjp(gelu_exact, pre_act)
    act_low = activated.astype(half)
    mlp_out = jnp.dot(act_low, down_weight, preferred_element_type=single) + down_bias.astype(
        single
    )
    result = after_attn + mlp_scale * mlp_out
    output = from_windows(
        result.reshape(window_count, WIN * WIN, channels), images, height, columns
    ).astype(half)
    grad_res = to_windows(cotangent).reshape(-1, channels).astype(single)
    grad_mlp = (grad_res * mlp_scale).astype(half)
    grad_down_w = jnp.dot(act_low.T, grad_mlp, preferred_element_type=single)
    grad_down_b = jnp.sum(grad_mlp.astype(single), axis=0)
    grad_act = jnp.dot(grad_mlp, down_weight.T, preferred_element_type=single)
    grad_pre = act_back(grad_act)[0].astype(half)
    grad_up_w = jnp.dot(hidden_two.T, grad_pre, preferred_element_type=single)
    grad_up_b = jnp.sum(grad_pre.astype(single), axis=0)
    grad_hidden_two = jnp.dot(grad_pre, up_weight.T, preferred_element_type=single)
    grad_after, grad_mid_gain, grad_mid_shift = norm_two_back(grad_hidden_two)
    grad_after = grad_after + grad_res
    grad_attn = (grad_after * attn_scale).astype(half)
    grad_out_w = jnp.dot(mixed.T, grad_attn, preferred_element_type=single)
    grad_out_b = jnp.sum(grad_attn.astype(single), axis=0)
    grad_mixed = (
        jnp.dot(grad_attn, out_weight.T, preferred_element_type=single)
        .astype(half)
        .reshape(heads_shape)
    )
    again = jnp.exp(attention_scores(queries, keys_all) - log_total)
    again_low = again.astype(half)
    grad_vals = jnp.einsum("whqk,wqhd->wkhd", again_low, grad_mixed, preferred_element_type=single)
    grad_probs = jnp.einsum("wqhd,wkhd->whqk", grad_mixed, vals_all, preferred_element_type=single)
    grad_scores = (
        again * (grad_probs - jnp.sum(again * grad_probs, axis=-1, keepdims=True))
    ).astype(half)
    grad_queries = (
        jnp.einsum("whqk,wkhd->wqhd", grad_scores, keys_all, preferred_element_type=single) * factor
    )
    grad_keys = (
        jnp.einsum("whqk,wqhd->wkhd", grad_scores, queries, preferred_element_type=single) * factor
    )
    grad_proj = jnp.concatenate(
        [
            grad_queries.reshape(-1, channels),
            grad_keys.reshape(-1, channels),
            grad_vals.reshape(-1, channels),
        ],
        axis=1,
    ).astype(half)
    grad_pairs = jnp.sum(grad_scores.astype(single), axis=0).reshape(HEADS, -1).T
    grad_table = jnp.dot(
        onehot.astype(single).T,
        grad_pairs,
        precision=lax.Precision.HIGHEST,
        preferred_element_type=single,
    )
    grad_in_w = jnp.dot(hidden_one.T, grad_proj, preferred_element_type=single)
    column_sums = jnp.sum(grad_proj.astype(single), axis=0)
    grad_in_b = jnp.concatenate([column_sums[:channels], column_sums[2 * channels :]])
    grad_hidden_one = jnp.dot(grad_proj, in_weight.T, preferred_element_type=single)
    grad_inputs, grad_pre_gain, grad_pre_shift = norm_one_back(grad_hidden_one * valid_tok)
    grad_tokens = grad_inputs + grad_after
    grad_shifted = from_windows(
        grad_tokens.reshape(window_count, WIN * WIN, channels), images, height, columns
    )
    grad_ext = jnp.roll(grad_shifted, SHIFT, axis=2)
    received = passed_along(grad_ext[:, height - SHIFT :].astype(jnp.bfloat16), "rows", 1).astype(
        jnp.float32
    )
    grad_patches = jnp.concatenate([received, grad_ext[:, : height - SHIFT]], axis=1)
    summed = lax.psum(
        (
            grad_pre_gain,
            grad_pre_shift,
            grad_in_w,
            grad_in_b,
            grad_table,
            grad_out_w,
            grad_out_b,
            grad_mid_gain,
            grad_mid_shift,
            grad_up_w,
            grad_up_b,
            grad_down_w,
            grad_down_b,
        ),
        ("rows", "batch"),
    )
    (
        grad_pre_gain,
        grad_pre_shift,
        grad_in_w,
        grad_in_b,
        grad_table,
        grad_out_w,
        grad_out_b,
        grad_mid_gain,
        grad_mid_shift,
        grad_up_w,
        grad_up_b,
        grad_down_w,
        grad_down_b,
    ) = summed
    return (
        output,
        grad_patches,
        grad_pre_gain,
        grad_pre_shift,
        grad_in_w,
        grad_in_b,
        grad_table,
        grad_out_w,
        grad_out_b,
        grad_mid_gain,
        grad_mid_shift,
        grad_up_w,
        grad_up_b,
        grad_down_w,
        grad_down_b,
    )


def solution(mesh):
    placed = (
        P("batch", "rows", None, None),
        P("batch"),
        P("batch", None),
        P(),
        P(),
        P(),
        P(),
        P(),
        P(),
        P(),
        P(),
        P(),
        P(),
        P(),
        P(),
        P(),
        P("batch", "rows", None, None),
    )
    return jax.shard_map(
        on_device,
        mesh=mesh,
        in_specs=placed,
        out_specs=(
            P("batch", "rows", None, None),
            P("batch", "rows", None, None),
            P(),
            P(),
            P(),
            P(),
            P(),
            P(),
            P(),
            P(),
            P(),
            P(),
            P(),
            P(),
            P(),
        ),
        check_vma=False,
    )
```

profile of v0, /device:TPU:0, one launch (start us, length us, event | category | flops | bytes accessed | tf_op | source)
XLA Modules:
  0.0 470.4 jit_solution(2767004228691779280)
XLA Ops:
  9.2 6.0 %collective-permute-start = (bf16[4,3,56,384]{3,2,1,0:T(8,128)(2,1)}, bf16[4,3,56,384]{3,2,1,0:T(8,128)(2,1)S(1)}, u32[]{:S(2)}, u32[]{:S(2)}) collective-permute-start(bf16[4,3,56,384]{3,2,1,0:T(8,128)(2,1)} %slice.60), channel_id=1, source_target_pairs={{0,28},{4,0},{8,4},{12,8},{16,12},{20,16},{24,20},{28,24},{1,29},{... | collective-permute-start | bytes 1548296 | tf_op jit(solution)/shard_map/ppermute | solution.py:20
  32.0 3.8 reshape.413
  53.5 4.2 fusion.7
  66.4 11.1 %reshape.403 = bf16[32,49,12,32]{1,0,3,2:T(8,128)(2,1)} reshape(bf16[1568,384]{0,1:T(8,128)(2,1)} %copy.122) | data formatting | bytes 2408448 | tf_op jit(solution)/shard_map/reshape | solution.py:138
  77.6 11.2 %reshape.405 = bf16[32,49,12,32]{1,0,3,2:T(8,128)(2,1)} reshape(bf16[1568,384]{0,1:T(8,128)(2,1)} %copy.124) | data formatting | bytes 2408448 | tf_op jit(solution)/shard_map/reshape | solution.py:137
  88.7 10.6 %reshape.404 = bf16[32,49,12,32]{1,0,3,2:T(8,128)(2,1)} reshape(bf16[1568,384]{0,1:T(8,128)(2,1)S(1)} %copy.123) | data formatting | bytes 2408448 | tf_op jit(solution)/shard_map/reshape | solution.py:136
  99.3 9.9 %fusion.62 = (f32[32,12,49]{2,1,0:T(8,128)S(1)}, f32[32,12,49,49]{2,3,1,0:T(8,128)S(1)}) fusion(f32[32,49,49]{1,2,0:T(8,128)S(1)} %compare_select_fusion, f32[12,49,49]{1,2,0:T(8,128)} %copy.127, bf16[32,49,12,32]{1,0,3,2:T(8,128)(2,1)} %reshape.405, bf16[32,49,12,32]{1,0,3,2:T(8,128)(2,1)} %reshape.404), kind=kOutput, calls=%fused_computation.143 | convolution fusion | flops 62676096 | bytes 6594224 | tf_op jit(solution)/shard_map/wqhd,wkhd->whqk/dot_general | solution.py:117
  114.0 4.7 convert_bitcast_fusion.1
  118.7 3.8 copy.133
  122.5 5.8 %convert_element_type.199 = bf16[1568,384]{0,1:T(8,128)(2,1)S(1)} reshape(bf16[32,49,12,32]{1,0,3,2:T(8,128)(2,1)} %copy.133) | data formatting | bytes 2408448 | tf_op jit(solution)/shard_map/convert_element_type | solution.py:145
  131.8 26.3 %multiply_convert_fusion.1 = (bf16[1568,1536]{1,0:T(8,128)(2,1)}, f32[1568,1536]{1,0:T(8,128)}, f32[1568,1536]{1,0:T(8,128)}) fusion(f32[1536]{0:T(1024)S(1)} %convert_element_type.204, bf16[384,1536]{1,0:T(8,128)(2,1)S(1)} %copy-done, f32[1568,384]{1,0:T(8,128)S(1)} %get-tuple-element.104, f32[384]{0:T(512)S(1)} %convert_element_type.202, ...), kind=kOutput, calls=%fused_computation.11 | convolution fusion | flops 2011656192 | bytes 27694336 | tf_op jit(solution)/shard_map/dot_general | solution.py:153
  158.1 9.8 %convert_reduce_fusion.1 = (f32[1536]{0:T(1024)S(1)}, bf16[1568,1536]{1,0:T(8,128)(2,1)S(1)}) fusion(f32[1568,1536]{1,0:T(8,128)} %get-tuple-element.88, f32[1568,1536]{1,0:T(8,128)} %get-tuple-element.105, bf16[1536,384]{1,0:T(8,128)(2,1)S(1)} %copy-done.44, f32[1568,384]{1,0:T(8,128)S(1)} %copy-done.9, f32[1568]{0:T(1024)S(1)} %mul.295), kind=kOutput, calls=%fused_computation.9 | convolution fusion | flops 1889425920 | bytes 27684992 | tf_op jit(solution)/shard_map/dot_general | solution.py:167
  167.9 3.9 fusion.55
  183.0 10.6 %reshape.406 = bf16[32,49,12,32]{1,0,3,2:T(8,128)(2,1)} reshape(bf16[1568,384]{0,1:T(8,128)(2,1)S(1)} %copy.137) | data formatting | bytes 2408448 | tf_op jit(solution)/shard_map/reshape | solution.py:180
  193.6 10.7 %convert_bitcast_fusion = bf16[32,49,12,32]{1,3,2,0:T(8,128)(2,1)} fusion(bf16[32,49,12,32]{1,0,3,2:T(8,128)(2,1)} %reshape.406, f32[32,12,49,49]{2,3,1,0:T(8,128)} %copy-done.1, f32[32,12,49]{2,1,0:T(8,128)S(1)} %log_add_fusion), kind=kOutput, calls=%fused_computation.36 | convolution fusion | flops 61453056 | bytes 6171648 | tf_op jit(solution)/shard_map/whqk,wqhd->wkhd/dot_general | solution.py:184
  204.2 13.3 %multiply_reduce_fusion = (f32[32,12,49]{2,1,0:T(8,128)S(1)}, f32[32,12,49,49]{2,3,1,0:T(8,128)}) fusion(f32[32,12,49,49]{2,3,1,0:T(8,128)} %copy-done.1, f32[32,12,49]{2,1,0:T(8,128)S(1)} %log_add_fusion, bf16[32,49,12,32]{1,0,3,2:T(8,128)(2,1)S(1)} %copy-done.4, bf16[32,49,12,32]{1,0,3,2:T(8,128)(2,1)S(1)} %copy-done.5), kind=kOutput, calls=%fused_computation.3 | convolution fusion | flops 61754112 | bytes 9934848 | tf_op jit(solution)/shard_map/wqhd,wkhd->whqk/dot_general | solution.py:185
  217.5 10.1 %convert_reduce_fusion = (f32[12,49,49]{1,2,0:T(8,128)}, bf16[32,12,49,49]{2,3,1,0:T(8,128)(2,1)S(1)}) fusion(f32[32,12,49,49]{2,3,1,0:T(8,128)} %get-tuple-element.108, f32[32,12,49]{2,1,0:T(8,128)S(1)} %get-tuple-element.107, f32[32,12,49,49]{2,3,1,0:T(8,128)} %copy-done.1, f32[32,12,49]{2,1,0:T(8,128)S(1)} %log_add_fusion), kind=kLoop, calls=%fused_computation.1 | loop fusion | flops 5503092 | bytes 9485616 | tf_op jit(solution)/shard_map/reduce_sum | solution.py:203
  227.7 5.0 %fusion.9 = bf16[32,49,12,32]{1,3,2,0:T(8,128)(2,1)} fusion(bf16[32,12,49,49]{2,3,1,0:T(8,128)(2,1)S(1)} %get-tuple-element.82, bf16[32,49,12,32]{1,0,3,2:T(8,128)(2,1)S(1)} %copy-done.7), kind=kOutput, calls=%fused_computation.35 | convolution fusion | flops 60211200 | bytes 4252416 | tf_op jit(solution)/shard_map/whqk,wqhd->wkhd/dot_general | solution.py:193
  232.7 5.6 %fusion.8 = bf16[32,49,12,32]{1,3,2,0:T(8,128)(2,1)} fusion(bf16[32,12,49,49]{2,3,1,0:T(8,128)(2,1)S(1)} %get-tuple-element.82, bf16[32,49,12,32]{1,0,3,2:T(8,128)(2,1)S(1)} %copy-done.6), kind=kOutput, calls=%fused_computation.34 | convolution fusion | flops 60211200 | bytes 4252416 | tf_op jit(solution)/shard_map/whqk,wkhd->wqhd/dot_general | solution.py:190
  238.3 4.5 fusion.54
  242.8 3.7 copy.148
  246.5 5.7 %reshape.409 = bf16[1568,384]{0,1:T(8,128)(2,1)S(1)} reshape(bf16[32,49,12,32]{1,0,3,2:T(8,128)(2,1)} %copy.148) | data formatting | bytes 2408448 | tf_op jit(solution)/shard_map/reshape | solution.py:199
  252.3 5.6 %copy.142 = bf16[32,49,12,32]{1,0,3,2:T(8,128)(2,1)} copy(bf16[32,49,12,32]{1,3,2,0:T(8,128)(2,1)} %fusion.8) | data formatting | bytes 2408448 | tf_op jit(solution)/shard_map/mul | solution.py:190
  257.9 6.8 %reshape.407 = bf16[1568,384]{0,1:T(8,128)(2,1)} reshape(bf16[32,49,12,32]{1,0,3,2:T(8,128)(2,1)} %copy.142) | data formatting | bytes 2408448 | tf_op jit(solution)/shard_map/reshape | solution.py:197
  264.6 5.5 %copy.145 = bf16[32,49,12,32]{1,0,3,2:T(8,128)(2,1)} copy(bf16[32,49,12,32]{1,3,2,0:T(8,128)(2,1)} %fusion.9) | data formatting | bytes 2408448 | tf_op jit(solution)/shard_map/mul | solution.py:193
  270.2 6.6 %reshape.408 = bf16[1568,384]{0,1:T(8,128)(2,1)} reshape(bf16[32,49,12,32]{1,0,3,2:T(8,128)(2,1)} %copy.145) | data formatting | bytes 2408448 | tf_op jit(solution)/shard_map/reshape | solution.py:198
  280.9 4.1 fusion.56
  286.2 7.4 %multiply_reduce_fusion.2 = (f32[384]{0:T(512)S(1)}, f32[1568]{0:T(1024)S(1)}, f32[384]{0:T(512)S(1)}, f32[1568,384]{1,0:T(8,128)S(1)}) fusion(f32[1568,384]{1,0:T(8,128)} %reshape.412, f32[1568]{0:T(1024)S(1)} %copy-done.31, f32[1568]{0:T(1024)S(1)} %copy-done.29, f32[384]{0:T(512)S(1)} %copy-done.38, f32[1568]{0:T(1024)S(1)} %copy-done.35, ...), kind=kOutput, calls=%fused_computation.70 | convolution fusion | flops 1392682752 | bytes 9344000 | tf_op jit(solution)/shard_map/dot_general | solution.py:213
  298.1 3.7 reshape_reshape.2
  307.3 6.2 %fusion.14 = bf16[1568,384]{1,0:T(8,128)(2,1)} fusion(f32[1568,384]{1,0:T(8,128)S(1)} %copy-done.15, bf16[1568,1536]{1,0:T(8,128)(2,1)} %get-tuple-element.87, bf16[1536,384]{1,0:T(8,128)(2,1)S(1)} %copy-done.45, f32[384]{0:T(512)S(1)} %copy-done.40, f32[1568]{0:T(1024)S(1)} %mul.295), kind=kOutput, calls=%fused_computation.45 | convolution fusion | flops 1852096512 | bytes 9617024 | tf_op jit(solution)/shard_map/dot_general | solution.py:156
  330.0 46.1 %all-reduce = (f32[384]{0:T(512)}, f32[384]{0:T(512)}, f32[768]{0:T(1024)}, f32[169,12]{0,1:T(8,128)}, f32[384]{0:T(512)}, /*index=5*/f32[384]{0:T(512)}, f32[384]{0:T(512)}, f32[1536]{0:T(1024)}, f32[384]{0:T(512)}) all-reduce(f32[384]{0:T(512)S(1)} %get-tuple-element.62, ...), channel_id=1, replica_groups=mesh['rows'=8,'batch'=4] {'rows','batch'}, use_global_device_ids=true, to_apply=%region_12.13 | all-reduce | flops 6636 | bytes 53088 | tf_op jit(solution)/shard_map/psum | solution.py:224
  380.3 75.1 %all-reduce.4.cloned.1.call-done = (f32[384,1152]{1,0:T(8,128)}, f32[384,384]{1,0:T(8,128)}, f32[384,1536]{1,0:T(8,128)}, f32[1536,384]{1,0:T(8,128)}) async-done(((f32[384,1152]{1,0:T(8,128)}, f32[384,384]{1,0:T(8,128)}, f32[384,1536]{1,0:T(8,128)}, f32[1536,384]{1,0:T(8,128)}), (f32[384,1152]{1,0:T(8,128)}, f32[384,384]{1,0:T(8,128)}, f32[384,1536]{1,0:T(8,128)}, ...) | async-done | bytes 7077904 | tf_op jit(solution)/shard_map/psum | solution.py:224
  (207 shorter events, 107.8 us)
Async XLA Ops:
  7.2 124.6 %copy-start = (bf16[384,1536]{1,0:T(8,128)(2,1)S(1)}, bf16[384,1536]{1,0:T(8,128)(2,1)}, u32[]{:S(2)}) copy-start(bf16[384,1536]{1,0:T(8,128)(2,1)} %param.29) | copy-start | bytes 3538948
  7.2 15.5 %copy-start.39 = (bf16[1536]{0:T(1024)(128)(2,1)S(1)}, bf16[1536]{0:T(1024)(128)(2,1)}, u32[]{:S(2)}) copy-start(bf16[1536]{0:T(1024)(128)(2,1)} %param.30) | copy-start | bytes 9220
  7.2 16.0 %copy-start.43 = (s32[4]{0:T(128)S(1)}, s32[4]{0:T(128)}, u32[]{:S(2)}) copy-start(s32[4]{0:T(128)} %param.18) | copy-start | bytes 52
  7.2 16.3 %copy-start.48 = (bf16[169,12]{0,1:T(8,128)(2,1)S(1)}, bf16[169,12]{0,1:T(8,128)(2,1)}, u32[]{:S(2)}) copy-start(bf16[169,12]{0,1:T(8,128)(2,1)} %param.24) | copy-start | bytes 12172
  7.2 448.2 %all-reduce.4.cloned.1.call-start = ((), (), s32[]{:S(2)}) async-start(), calls=%async_computation | async-start | bytes 14155776 | tf_op jit(solution)/shard_map/psum | solution.py:224
  9.2 29.6 %collective-permute-start = (bf16[4,3,56,384]{3,2,1,0:T(8,128)(2,1)}, bf16[4,3,56,384]{3,2,1,0:T(8,128)(2,1)S(1)}, u32[]{:S(2)}, u32[]{:S(2)}) collective-permute-start(bf16[4,3,56,384]{3,2,1,0:T(8,128)(2,1)} %slice.60), channel_id=1, source_target_pairs={{0,28},{4,0},{8,4},{12,8},{16,12},{20,16},{24,20},{28,24},{1,29},{... | collective-permute-start | bytes 1548296 | tf_op jit(solution)/shard_map/ppermute | solution.py:20
  17.9 35.6 %copy-start.37 = (f32[384]{0:T(512)}, f32[384]{0:T(512)S(1)}, u32[]{:S(2)}) copy-start(f32[384]{0:T(512)S(1)} %convert_element_type.187) | copy-start | bytes 4612
  19.2 34.2 %copy-start.41 = (f32[384]{0:T(512)}, f32[384]{0:T(512)S(1)}, u32[]{:S(2)}) copy-start(f32[384]{0:T(512)S(1)} %convert_element_type.188) | copy-start | bytes 4612
  23.6 29.9 %copy-start.34 = (f32[1568]{0:T(1024)}, f32[1568]{0:T(1024)S(1)}, u32[]{:S(2)}) copy-start(f32[1568]{0:T(1024)S(1)} %transpose.110) | copy-start | bytes 18820
  48.9 4.5 copy-start.28
  49.8 3.7 copy-start.26
  49.8 3.7 copy-start.30
  49.8 3.7 copy-start.46
  109.2 4.8 %copy-start.1 = (f32[32,12,49,49]{2,3,1,0:T(8,128)}, f32[32,12,49,49]{2,3,1,0:T(8,128)S(1)}, u32[]{:S(2)}) copy-start(f32[32,12,49,49]{2,3,1,0:T(8,128)S(1)} %get-tuple-element.102) | copy-start | bytes 11063812
  109.3 4.8 %copy-start.3 = (bf16[32,49,12,32]{1,0,3,2:T(8,128)(2,1)S(1)}, bf16[32,49,12,32]{1,0,3,2:T(8,128)(2,1)}, u32[]{:S(2)}) copy-start(bf16[32,49,12,32]{1,0,3,2:T(8,128)(2,1)} %reshape.403) | copy-start | bytes 3612676
  122.5 5.8 %copy-start.23 = (bf16[384,384]{1,0:T(8,128)(2,1)S(1)}, bf16[384,384]{1,0:T(8,128)(2,1)}, u32[]{:S(2)}) copy-start(bf16[384,384]{1,0:T(8,128)(2,1)} %param.25) | copy-start | bytes 884740
  131.2 44.0 %copy-start.14 = (f32[1568,384]{1,0:T(8,128)}, f32[1568,384]{1,0:T(8,128)S(1)}, u32[]{:S(2)}) copy-start(f32[1568,384]{1,0:T(8,128)S(1)} %get-tuple-element.104) | copy-start | bytes 7225348
  131.8 26.3 %copy-start.9 = (f32[1568,384]{1,0:T(8,128)S(1)}, f32[1568,384]{1,0:T(8,128)}, u32[]{:S(2)}) copy-start(f32[1568,384]{1,0:T(8,128)} %reshape.413) | copy-start | bytes 7225348
  131.8 26.3 %copy-start.44 = (bf16[1536,384]{1,0:T(8,128)(2,1)S(1)}, bf16[1536,384]{1,0:T(8,128)(2,1)}, u32[]{:S(2)}) copy-start(bf16[1536,384]{1,0:T(8,128)(2,1)} %param.31) | copy-start | bytes 3538948
  193.6 10.7 %copy-start.4 = (bf16[32,49,12,32]{1,0,3,2:T(8,128)(2,1)S(1)}, bf16[32,49,12,32]{1,0,3,2:T(8,128)(2,1)}, u32[]{:S(2)}) copy-start(bf16[32,49,12,32]{1,0,3,2:T(8,128)(2,1)} %reshape.403) | copy-start | bytes 3612676
  193.6 10.7 %copy-start.5 = (bf16[32,49,12,32]{1,0,3,2:T(8,128)(2,1)S(1)}, bf16[32,49,12,32]{1,0,3,2:T(8,128)(2,1)}, u32[]{:S(2)}) copy-start(bf16[32,49,12,32]{1,0,3,2:T(8,128)(2,1)} %reshape.406) | copy-start | bytes 3612676
  217.5 10.1 %copy-start.7 = (bf16[32,49,12,32]{1,0,3,2:T(8,128)(2,1)S(1)}, bf16[32,49,12,32]{1,0,3,2:T(8,128)(2,1)}, u32[]{:S(2)}) copy-start(bf16[32,49,12,32]{1,0,3,2:T(8,128)(2,1)} %reshape.404) | copy-start | bytes 3612676
  227.7 5.0 %copy-start.6 = (bf16[32,49,12,32]{1,0,3,2:T(8,128)(2,1)S(1)}, bf16[32,49,12,32]{1,0,3,2:T(8,128)(2,1)}, u32[]{:S(2)}) copy-start(bf16[32,49,12,32]{1,0,3,2:T(8,128)(2,1)} %reshape.405) | copy-start | bytes 3612676
  227.7 10.6 %slice-start = ((s8[4816896]{0:T(1024)(128)(4,1)}), s8[622592]{0:T(1024)(128)(4,1)S(1)}, s32[]{:S(2)}) async-start(s8[4816896]{0:T(1024)(128)(4,1)} %bitcast.101), calls=%async_computation.1 | async-start | bytes 1245184
  232.7 5.6 %copy-start.10 = (f32[1568,384]{1,0:T(8,128)S(1)}, f32[1568,384]{1,0:T(8,128)}, u32[]{:S(2)}) copy-start(f32[1568,384]{1,0:T(8,128)} %reshape.413) | copy-start | bytes 7225348
  232.7 5.6 %slice-start.1 = ((s8[4816896]{0:T(1024)(128)(4,1)}), s8[4194304]{0:T(1024)(128)(4,1)S(1)}, s32[]{:S(2)}) async-start(s8[4816896]{0:T(1024)(128)(4,1)} %bitcast.101), calls=%async_computation.2 | async-start | bytes 8388608
  238.3 4.6 copy-start.18
  286.2 7.4 %copy-start.27 = (f32[1568]{0:T(1024)S(1)}, f32[1568]{0:T(1024)}, u32[]{:S(2)}) copy-start(f32[1568]{0:T(1024)} %copy-done.26) | copy-start | bytes 18820
  286.2 7.5 %copy-start.13 = (f32[1568,384]{1,0:T(8,128)S(1)}, f32[1568,384]{1,0:T(8,128)}, u32[]{:S(2)}) copy-start(f32[1568,384]{1,0:T(8,128)} %reshape.412) | copy-start | bytes 7225348
  326.3 3.7 copy-start.36
  326.3 49.8 %collective-permute-start.1 = (bf16[4,3,56,384]{3,0,2,1:T(4,128)(2,1)}, bf16[4,3,56,384]{3,0,2,1:T(4,128)(2,1)}, u32[]{:S(2)}, u32[]{:S(2)}) collective-permute-start(bf16[4,3,56,384]{3,0,2,1:T(4,128)(2,1)} %fusion.45), channel_id=1, source_target_pairs={{0,4},{4,8},{8,12},{12,16},{16,20},{20,24},{24,28},{28,0},{1,5},{5... | collective-permute-start | bytes 1548296 | tf_op jit(solution)/shard_map/ppermute | solution.py:20
  455.4 3.8 copy-start.22
  (22 other events, 46.3 us)
Sparse Core Ops, SparseCore 0:
  285.1 170.2 all-reduce.3
where the time goes:
time: 475 us; the launch traced here: 470 us
  local copies, waits for them, and re-layouts  160 us (34%)
  matrix products  127 us (27%)
  waiting for transfers between devices  75.1 us (16%)
  blocking collectives  46.1 us (10%)
  other arithmetic  41 us (9%)
  between operations  15.3 us (3%)
  starting transfers between devices  6.07 us (1%)
    psum x1, waiting for transfers between devices, on_device(): lax.psum((grad_pre_gain, grad_pre_shift, grad_in_w, grad_in_b, grad_table...  75.1 us
    psum x1, blocking collectives, on_device(): lax.psum((grad_pre_gain, grad_pre_shift, grad_in_w, grad_in_b, grad_table...  46.1 us
    dot_general x1, matrix products, on_device(): jnp.dot(hidden_two, up_weight, preferred_element_type=single)  26.3 us
    unnamed x110, local copies, waits for them, and re-layouts  21.6 us
    dot_general x1, matrix products, on_device(): jnp.einsum('wqhd,wkhd->whqk', grad_mixed, vals_all, preferred_element_typ...  13.3 us
    reshape x1, local copies, waits for them, and re-layouts, on_device(): projected[:, channels:2 * channels].astype(half).reshape(heads_shape)  11.2 us
    reshape x1, local copies, waits for them, and re-layouts, on_device(): vals_all = projected[:, 2 * channels:].astype(half).reshape(heads_shape)  11.1 us
    dot_general x1, matrix products, on_device(): jnp.einsum('whqk,wqhd->wkhd', again_low, grad_mixed, preferred_element_ty...  10.7 us
  transfers between devices with their start and end apart: 3, of which 1 were waited for; matrix products, arithmetic and copies ran while one was open for 14% of the time, Pallas kernels for 0%

commit v1 on v0

v1 whole, which is shorter than its diff:
```python
import math

import jax
import jax.numpy as jnp
from jax import lax
from jax.experimental import pallas as pl
from jax.experimental.pallas import tpu as pltpu
from jax.sharding import PartitionSpec as P

HEADS = 12
WIN = 7
SHIFT = 3
TOK = WIN * WIN
PAD = 56
GROUP = 4

EPSILON = 1e-05
KEEP_RATE = 0.8
MASKED = -100.0
EMPTY = -1e30

F32 = jnp.float32
BF16 = jnp.bfloat16


def nn(a, b):
    return lax.dot_general(a, b, (((1,), (0,)), ((), ())), preferred_element_type=F32)


def nt(a, b):
    return lax.dot_general(a, b, (((1,), (1,)), ((), ())), preferred_element_type=F32)


def tn(a, b):
    return lax.dot_general(a, b, (((0,), (0,)), ((), ())), preferred_element_type=F32)


def col_sum(a):
    return jnp.sum(a, axis=0, keepdims=True)


def row_mean(a):
    return jnp.mean(a, axis=-1, keepdims=True)


def normed(v):
    centred = v - row_mean(v)
    root = lax.rsqrt(row_mean(centred * centred) + EPSILON)
    return centred * root, root


def head_masks():
    lane = lax.broadcasted_iota(jnp.int32, (PAD, 128), 1)
    return [(lane >= 32 * h) & (lane < 32 * (h + 1)) for h in range(GROUP)]


def stacked(pair, masks):
    a, b = pair[:PAD], pair[PAD:]
    rows = [
        jnp.concatenate([jnp.where(m, a, 0.0), jnp.where(m, b, 0.0)], axis=1) for m in masks
    ]
    return jnp.concatenate(rows, axis=0).astype(BF16)


def diagonal(pair):
    a, b = pair[:PAD], pair[PAD:]
    z = jnp.zeros_like(a)
    return jnp.concatenate(
        [jnp.concatenate([a, z], axis=1), jnp.concatenate([z, b], axis=1)], axis=0
    ).astype(BF16)


def undiagonal(m):
    return jnp.concatenate([m[:PAD, :128], m[PAD:, 128:]], axis=0)


def unstacked(m, masks):
    sides = []
    for side in range(2):
        total = None
        for h, mask in enumerate(masks):
            piece = jnp.where(mask, m[h * PAD : (h + 1) * PAD, side * 128 : (side + 1) * 128], 0.0)
            total = piece if total is None else total + piece
        sides.append(total)
    return jnp.concatenate(sides, axis=0)


def normal_cdf_pdf(v):
    e = jnp.exp(-0.5 * (v * v))
    t = 1.0 / (1.0 + (0.3275911 / math.sqrt(2.0)) * jnp.abs(v))
    poly = 1.061405429
    for c in (-1.453152027, 1.421413741, -0.284496736, 0.254829592):
        poly = poly * t + c
    half_tail = (0.5 * poly) * t * e
    cdf = jnp.where(v >= 0.0, 1.0 - half_tail, half_tail)
    return cdf, e * (1.0 / math.sqrt(2.0 * math.pi))


def forward_kernel(
    widths_ref,
    keep_ref,
    own_ref,
    halo_ref,
    cot_ref,
    p_own_ref,
    p_halo_ref,
    p_cot_ref,
    p_out_ref,
    col_ref,
    bias_ref,
    vec_ref,
    up_bias_ref,
    in_w_ref,
    out_w_ref,
    up_w_ref,
    down_w_ref,
    out_ref,
    xs_ref,
    qkv_ref,
    prob_ref,
    grad_after_ref,
    grad_mixed_ref,
    acc_ref,
    proj_sc,
    mixed_sc,
    down_sc,
):
    i = pl.program_id(0)
    last = pl.num_programs(0) - 1
    channels = own_ref.shape[-1]
    hidden = up_w_ref.shape[1]
    chunks = hidden // channels
    groups = channels // 128
    pairs = proj_sc.shape[0] // (2 * PAD)
    factor = 1.0 / math.sqrt(channels // HEADS)

    @pl.when(i == 0)
    def _():
        acc_ref[...] = jnp.zeros_like(acc_ref)
        down_sc[...] = jnp.zeros_like(down_sc)

    def vec(n):
        return vec_ref[n : n + 1, :]

    valid = (col_ref[...] < widths_ref[i]).astype(F32)
    ka = keep_ref[i, 0].astype(F32) / KEEP_RATE
    kb = keep_ref[i, 1].astype(F32) / KEEP_RATE
    valid_a = valid * ka
    valid_b = valid * kb

    xs = nn(p_own_ref[...], own_ref[0]) + nn(p_halo_ref[...], halo_ref[0])
    xs_ref[0] = xs.astype(BF16)
    norm_one, _ = normed(xs)
    hidden_one = ((norm_one * vec(0) + vec(1)) * valid).astype(BF16)
    for part in range(3):
        cols = slice(part * channels, (part + 1) * channels)
        projected = nn(hidden_one, in_w_ref[:, cols]) + vec(2 + part)
        proj_sc[:, cols] = projected
        qkv_ref[0, :, cols] = projected.astype(BF16)

    masks = head_masks()

    def one_pair(j, carry):
        rows = pl.ds(pl.multiple_of(j * 2 * PAD, 2 * PAD), 2 * PAD)
        edge = (j == pairs - 1).astype(jnp.int32)
        for g in range(groups):
            lanes = [
                slice(part * channels + g * 128, part * channels + (g + 1) * 128)
                for part in range(3)
            ]
            q = stacked(proj_sc[rows, lanes[0]], masks)
            k = diagonal(proj_sc[rows, lanes[1]])
            v = diagonal(proj_sc[rows, lanes[2]])
            scores = nt(k, q) * factor + bias_ref[edge, g]
            probs = []
            for side in (scores[:PAD], scores[PAD:]):
                e = jnp.exp(side - jnp.max(side, axis=0, keepdims=True))
                probs.append(e * (1.0 / col_sum(e)))
            probs = jnp.concatenate(probs, axis=0).astype(BF16)
            prob_ref[0, j, g] = probs
            mixed_sc[rows, lanes[0]] = unstacked(tn(probs, v), masks)
        return carry

    lax.fori_loop(0, pairs, one_pair, 0)

    mixed = mixed_sc[...].astype(BF16)
    after = xs + valid_a * (nn(mixed, out_w_ref[...]) + vec(5))
    norm_two, root_two = normed(after)
    hidden_two = (norm_two * vec(6) + vec(7)).astype(BF16)
    cot = nn(p_cot_ref[...], cot_ref[0])
    grad_mlp_wide = (cot * valid_b).astype(BF16)
    mlp = jnp.zeros_like(after)
    grad_hidden = jnp.zeros_like(after)
    up_base = hidden
    small = 2 * hidden + channels
    for c in range(chunks):
        cols = slice(c * channels, (c + 1) * channels)
        pre = nn(hidden_two, up_w_ref[:, cols]) + up_bias_ref[:, cols]
        cdf, pdf = normal_cdf_pdf(pre)
        act = (pre * cdf).astype(BF16)
        mlp = mlp + nn(act, down_w_ref[cols, :])
        grad_act = nt(grad_mlp_wide, down_w_ref[cols, :])
        grad_pre = (grad_act * (cdf + pre * pdf)).astype(BF16)
        grad_hidden = grad_hidden + nt(grad_pre, up_w_ref[:, cols])
        up_rows = slice(up_base + c * channels, up_base + (c + 1) * channels)
        acc_ref[up_rows, :] += tn(hidden_two, grad_pre)
        down_sc[:, cols] += tn(grad_mlp_wide, act)
        acc_ref[small + 4 + c : small + 5 + c, :] += col_sum(grad_pre.astype(F32))
    result = (after + valid_b * (mlp + vec(8))).astype(BF16)
    out_ref[0] = nn(p_out_ref[...], result).astype(BF16)

    d = grad_hidden * vec(6)
    grad_after = cot + root_two * (d - row_mean(d) - norm_two * row_mean(d * norm_two))
    grad_after_ref[0] = grad_after
    grad_attn = (grad_after * valid_a).astype(BF16)
    grad_mixed_ref[0] = nt(grad_attn, out_w_ref[...]).astype(BF16)
    acc_ref[2 * hidden : 2 * hidden + channels, :] += tn(mixed, grad_attn)
    acc_ref[small : small + 1, :] += col_sum(grad_hidden * norm_two)
    acc_ref[small + 1 : small + 2, :] += col_sum(grad_hidden)
    acc_ref[small + 2 : small + 3, :] += col_sum(grad_attn.astype(F32))
    acc_ref[small + 3 : small + 4, :] += col_sum(grad_mlp_wide.astype(F32))

    @pl.when(i == last)
    def _():
        for c in range(chunks):
            cols = slice(c * channels, (c + 1) * channels)
            acc_ref[cols, :] = down_sc[:, cols].T


def backward_kernel(
    widths_ref,
    xs_ref,
    qkv_ref,
    prob_ref,
    grad_after_ref,
    grad_mixed_ref,
    p_own_t_ref,
    p_halo_t_ref,
    col_ref,
    vec_ref,
    in_w_ref,
    grad_own_ref,
    grad_halo_ref,
    acc_ref,
    table_ref,
    proj_sc,
):
    i = pl.program_id(0)
    channels = xs_ref.shape[-1]
    groups = channels // 128
    pairs = proj_sc.shape[0] // (2 * PAD)
    factor = 1.0 / math.sqrt(channels // HEADS)

    @pl.when(i == 0)
    def _():
        acc_ref[...] = jnp.zeros_like(acc_ref)
        table_ref[...] = jnp.zeros_like(table_ref)

    def vec(n):
        return vec_ref[n : n + 1, :]

    valid = (col_ref[...] < widths_ref[i]).astype(F32)
    masks = head_masks()

    def one_pair(j, carry):
        rows = pl.ds(pl.multiple_of(j * 2 * PAD, 2 * PAD), 2 * PAD)
        for g in range(groups):
            lanes = [
                slice(part * channels + g * 128, part * channels + (g + 1) * 128)
                for part in range(3)
            ]
            pair_q = qkv_ref[0, rows, lanes[0]].astype(F32)
            pair_k = qkv_ref[0, rows, lanes[1]].astype(F32)
            pair_v = qkv_ref[0, rows, lanes[2]].astype(F32)
            pair_m = grad_mixed_ref[0, rows, lanes[0]].astype(F32)
            q = stacked(pair_q, masks)
            gm = stacked(pair_m, masks)
            k = diagonal(pair_k)
            v = diagonal(pair_v)
            probs_low = prob_ref[0, j, g]
            probs = probs_low.astype(F32)
            grad_v = undiagonal(nn(probs_low, gm))
            weighted = probs * nt(v, gm)
            scores = []
            for lo in (0, PAD):
                side = weighted[lo : lo + PAD]
                scores.append(side - probs[lo : lo + PAD] * col_sum(side))
            table_ref[g] += scores[0] + scores[1]
            grad_s = jnp.concatenate(scores, axis=0).astype(BF16)
            grad_k = undiagonal(nn(grad_s, q)) * factor
            grad_q = unstacked(tn(grad_s, k), masks) * factor
            proj_sc[rows, lanes[0]] = grad_q.astype(BF16)
            proj_sc[rows, lanes[1]] = grad_k.astype(BF16)
            proj_sc[rows, lanes[2]] = grad_v.astype(BF16)
        return carry

    lax.fori_loop(0, pairs, one_pair, 0)

    norm_one, root_one = normed(xs_ref[0].astype(F32))
    hidden_one = ((norm_one * vec(0) + vec(1)) * valid).astype(BF16)
    grad_hidden = jnp.zeros_like(norm_one)
    small = 3 * channels
    for part in range(3):
        cols = slice(part * channels, (part + 1) * channels)
        grad_proj = proj_sc[:, cols]
        acc_ref[cols, :] += tn(hidden_one, grad_proj)
        grad_hidden = grad_hidden + nt(grad_proj, in_w_ref[:, cols])
        if part != 1:
            row = small + 2 + part // 2
            acc_ref[row : row + 1, :] += col_sum(grad_proj.astype(F32))
    grad_hidden = grad_hidden * valid
    acc_ref[small : small + 1, :] += col_sum(grad_hidden * norm_one)
    acc_ref[small + 1 : small + 2, :] += col_sum(grad_hidden)
    d = grad_hidden * vec(0)
    grad_xs = grad_after_ref[0] + root_one * (
        d - row_mean(d) - norm_one * row_mean(d * norm_one)
    )
    high = grad_xs.astype(BF16)
    rest = (grad_xs - high.astype(F32)).astype(BF16)
    p_own_t = p_own_t_ref[...]
    grad_own_ref[0] = nn(p_own_t, high) + nn(p_own_t, rest)
    grad_halo_ref[0] = nn(p_halo_t_ref[...], high).astype(BF16)


def placements(height, columns):
    row = jnp.arange(columns // WIN * PAD, dtype=jnp.int32)
    place = row % PAD
    real = place < TOK
    s = jnp.where(real, place // WIN, 1000)
    t = row // PAD * WIN + place % WIN
    shifted = (t + SHIFT) % columns
    own = jnp.where(s < height - SHIFT, (s + SHIFT) * columns + shifted, -1)
    halo = jnp.where((s >= height - SHIFT) & real, (s - height + SHIFT) * columns + shifted, -1)
    plain = jnp.where(real, s * columns + t, -1)

    def hot(index, count, first=0):
        return index[:, None] == first + jnp.arange(count, dtype=jnp.int32)[None, :]

    def hot_t(index, count, first=0):
        return index[None, :] == first + jnp.arange(count, dtype=jnp.int32)[:, None]

    area = height * columns
    edge = SHIFT * columns
    mats = dict(
        own=hot(own, area),
        halo=hot(halo, edge),
        cot=hot(plain, area),
        out=hot_t(plain, area),
        own_t=hot_t(own, area - edge, edge),
        halo_t=hot_t(halo, edge),
    )
    col = jnp.where(real, shifted, 1 << 20)
    return {k: v.astype(BF16) for k, v in mats.items()}, col[:, None]


def pair_offsets():
    a = jnp.arange(TOK, dtype=jnp.int32)
    r, c = a // WIN, a % WIN
    span = 2 * WIN - 1
    index = (r[None, :] - r[:, None] + WIN - 1) * span + c[None, :] - c[:, None] + WIN - 1
    return index[None] == jnp.arange(span * span, dtype=jnp.int32)[:, None, None]


def score_bias(bias_table, last_row):
    hot = pair_offsets().astype(BF16).reshape(-1, TOK * TOK)
    bias = lax.dot_general(
        bias_table, hot, (((0,), (0,)), ((), ())), preferred_element_type=F32
    ).reshape(HEADS, TOK, TOK)
    a = jnp.arange(TOK, dtype=jnp.int32)
    cut = WIN - SHIFT
    row_region = (a // WIN >= cut) & last_row
    col_region = a % WIN >= cut
    row_same = row_region[:, None] == row_region[None, :]
    col_same = col_region[:, None] == col_region[None, :]
    inner = jnp.where(row_same, 0.0, MASKED).astype(F32)
    edge = jnp.where(row_same & col_same, 0.0, MASKED).astype(F32)

    def laid(mask):
        full = jnp.pad(
            bias + mask[None], ((0, 0), (0, 0), (0, PAD - TOK)), constant_values=0.0
        )
        full = jnp.pad(full, ((0, 0), (0, PAD - TOK), (0, 0)), constant_values=EMPTY)
        full = full.reshape(HEADS // GROUP, GROUP, PAD, PAD).transpose(0, 2, 1, 3)
        return full.reshape(HEADS // GROUP, PAD, GROUP * PAD)

    plain, right = laid(inner), laid(edge)
    return jnp.stack(
        [jnp.concatenate([plain, plain], axis=1), jnp.concatenate([plain, right], axis=1)]
    )


def whole(shape):
    return pl.BlockSpec(shape, lambda i: (0,) * len(shape), pipeline_mode=pl.Buffered(1))


def kept(shape):
    return pl.BlockSpec(shape, lambda i: (0,) * len(shape))


def by_image(shape):
    return pl.BlockSpec((1,) + shape, lambda i: (i,) + (0,) * len(shape))


def in_smem():
    return pl.BlockSpec(memory_space=pltpu.SMEM)


def power_bits(count):
    bits = count.bit_length() - 1
    assert 1 << bits == count
    return bits


def stage_orders(sizes):
    first = [("batch", 0)]
    rows = [("rows", b) for b in range(power_bits(sizes["rows"]))]
    batch = [("batch", b) for b in range(1, power_bits(sizes["batch"]))]
    lead = batch[:1] + rows[:2]
    rest = rows[2:] + batch[1:]
    orders = [lead[k:] + lead[:k] + rest for k in range(len(lead))]
    return first, orders


def swapped(value, axis, bit):
    count = lax.axis_size(axis)
    return lax.ppermute(value, axis, [(n, n ^ (1 << bit)) for n in range(count)])


def my_bit(axis, bit):
    return (lax.axis_index(axis) >> bit) & 1


def halved(value, stage):
    half = value.shape[0] // 2
    bit = my_bit(*stage)
    sent = lax.dynamic_slice_in_dim(value, (1 - bit) * half, half).astype(BF16)
    keep = lax.dynamic_slice_in_dim(value, bit * half, half)
    return keep + swapped(sent, *stage).astype(F32)


def doubled(value, stage):
    other = swapped(value, *stage)
    bit = my_bit(*stage)
    return jnp.where(
        bit == 0, jnp.concatenate([value, other]), jnp.concatenate([other, value])
    )


def summed_over_devices(value, cuts, sizes):
    first, orders = stage_orders(sizes)
    parts, start = [], 0
    for rows in cuts:
        parts.append(value[start : start + rows])
        start += rows
    for stage in first:
        parts = [halved(p, stage) for p in parts]
    for step in range(len(orders[0])):
        parts = [halved(p, orders[n % len(orders)][step]) for n, p in enumerate(parts)]
    parts = [p.astype(BF16) for p in parts]
    for step in reversed(range(len(orders[0]))):
        parts = [doubled(p, orders[n % len(orders)][step]) for n, p in enumerate(parts)]
    for stage in first:
        parts = [doubled(p, stage) for p in parts]
    return parts


def on_device(sizes, interpret, *args):
    (
        patches,
        widths,
        keep_mask,
        pre_gain,
        pre_shift,
        in_weight,
        in_bias,
        bias_table,
        out_weight,
        out_bias,
        mid_gain,
        mid_shift,
        up_weight,
        up_bias,
        down_weight,
        down_bias,
        cotangent,
    ) = args
    images, height, columns, channels = patches.shape
    hidden = up_weight.shape[1]
    area = height * columns
    edge = SHIFT * columns
    count = lax.axis_size("rows")
    padded = columns // WIN * PAD
    pairs = columns // WIN // 2
    groups = channels // 128
    chunks = hidden // channels

    halo = lax.ppermute(
        patches[:, :SHIFT].reshape(images, edge, channels),
        "rows",
        [(n, (n - 1) % count) for n in range(count)],
    )
    own = patches.reshape(images, area, channels)
    cot = cotangent.reshape(images, area, channels)
    mats, col = placements(height, columns)
    bias = score_bias(bias_table, lax.axis_index("rows") == count - 1)
    zero = jnp.zeros((channels,), F32)
    vecs = jnp.stack(
        [
            pre_gain.astype(F32),
            pre_shift.astype(F32),
            in_bias[:channels].astype(F32),
            zero,
            in_bias[channels:].astype(F32),
            out_bias.astype(F32),
            mid_gain.astype(F32),
            mid_shift.astype(F32),
            down_bias.astype(F32),
        ]
        + [zero] * 7
    )
    grid = (images,)
    params = pltpu.CompilerParams(
        dimension_semantics=("arbitrary",), vmem_limit_bytes=60 * 1024 * 1024
    )
    rows_one = 2 * hidden + channels + 128
    rows_two = 3 * channels + 128
    output, xs, qkv, probs, grad_after, grad_mixed, acc_one = pl.pallas_call(
        forward_kernel,
        grid=grid,
        in_specs=[
            in_smem(),
            in_smem(),
            by_image((area, channels)),
            by_image((edge, channels)),
            by_image((area, channels)),
            whole((padded, area)),
            whole((padded, edge)),
            whole((padded, area)),
            whole((area, padded)),
            whole((padded, 1)),
            whole(bias.shape),
            whole((16, channels)),
            whole((1, hidden)),
            whole((channels, 3 * channels)),
            whole((channels, channels)),
            whole((channels, hidden)),
            whole((hidden, channels)),
        ],
        out_specs=[
            by_image((area, channels)),
            by_image((padded, channels)),
            by_image((padded, 3 * channels)),
            by_image((pairs, groups, 2 * PAD, GROUP * PAD)),
            by_image((padded, channels)),
            by_image((padded, channels)),
            kept((rows_one, channels)),
        ],
        out_shape=[
            jax.ShapeDtypeStruct((images, area, channels), BF16),
            jax.ShapeDtypeStruct((images, padded, channels), BF16),
            jax.ShapeDtypeStruct((images, padded, 3 * channels), BF16),
            jax.ShapeDtypeStruct((images, pairs, groups, 2 * PAD, GROUP * PAD), BF16),
            jax.ShapeDtypeStruct((images, padded, channels), F32),
            jax.ShapeDtypeStruct((images, padded, channels), BF16),
            jax.ShapeDtypeStruct((rows_one, channels), F32),
        ],
        scratch_shapes=[
            pltpu.VMEM((padded, 3 * channels), F32),
            pltpu.VMEM((padded, channels), F32),
            pltpu.VMEM((channels, hidden), F32),
        ],
        compiler_params=params,
        interpret=interpret,
        name="forward_mlp",
    )(
        widths,
        keep_mask,
        own,
        halo,
        cot,
        mats["own"],
        mats["halo"],
        mats["cot"],
        mats["out"],
        col,
        bias,
        vecs,
        up_bias.astype(F32)[None, :],
        in_weight,
        out_weight,
        up_weight,
        down_weight,
    )
    grad_own, grad_halo, acc_two, table = pl.pallas_call(
        backward_kernel,
        grid=grid,
        in_specs=[
            in_smem(),
            by_image((padded, channels)),
            by_image((padded, 3 * channels)),
            by_image((pairs, groups, 2 * PAD, GROUP * PAD)),
            by_image((padded, channels)),
            by_image((padded, channels)),
            whole((area - edge, padded)),
            whole((edge, padded)),
            whole((padded, 1)),
            whole((16, channels)),
            whole((channels, 3 * channels)),
        ],
        out_specs=[
            by_image((area - edge, channels)),
            by_image((edge, channels)),
            kept((rows_two, channels)),
            kept((groups, PAD, GROUP * PAD)),
        ],
        out_shape=[
            jax.ShapeDtypeStruct((images, area - edge, channels), F32),
            jax.ShapeDtypeStruct((images, edge, channels), BF16),
            jax.ShapeDtypeStruct((rows_two, channels), F32),
            jax.ShapeDtypeStruct((groups, PAD, GROUP * PAD), F32),
        ],
        scratch_shapes=[pltpu.VMEM((padded, 3 * channels), BF16)],
        compiler_params=params,
        interpret=interpret,
        name="attention_back",
    )(
        widths,
        xs,
        qkv,
        probs,
        grad_after,
        grad_mixed,
        mats["own_t"],
        mats["halo_t"],
        col,
        vecs,
        in_weight,
    )
    received = lax.ppermute(grad_halo, "rows", [(n, (n + 1) % count) for n in range(count)])
    grad_patches = jnp.concatenate([received.astype(F32), grad_own], axis=1).reshape(
        images, height, columns, channels
    )
    pairs_grad = table.reshape(groups, PAD, GROUP, PAD)[:, :TOK, :, :TOK]
    pairs_grad = pairs_grad.transpose(0, 2, 1, 3).reshape(HEADS, TOK * TOK)
    grad_table = lax.dot_general(
        pair_offsets().astype(F32).reshape(-1, TOK * TOK),
        pairs_grad,
        (((1,), (1,)), ((), ())),
        precision=lax.Precision.HIGHEST,
        preferred_element_type=F32,
    )
    table_size = grad_table.size
    table_rows = -(-table_size // channels)
    flat = jnp.pad(grad_table.reshape(-1), (0, table_rows * channels - table_size))
    small_two = 3 * channels
    acc_two = lax.dynamic_update_slice(acc_two, flat.reshape(table_rows, channels), (small_two + 4, 0))

    one = jnp.concatenate(summed_over_devices(acc_one, (1280, 1280, 1024), sizes)).astype(F32)
    two = jnp.concatenate(summed_over_devices(acc_two, (512, 768), sizes)).astype(F32)
    grad_down_w = one[:hidden]
    grad_up_w = jnp.concatenate(
        [one[hidden + c * channels : hidden + (c + 1) * channels] for c in range(chunks)], axis=1
    )
    grad_out_w = one[2 * hidden : 2 * hidden + channels]
    s = 2 * hidden + channels
    grad_in_w = jnp.concatenate(
        [two[c * channels : (c + 1) * channels] for c in range(3)], axis=1
    )
    return (
        output.reshape(images, height, columns, channels),
        grad_patches,
        two[small_two],
        two[small_two + 1],
        grad_in_w,
        jnp.concatenate([two[small_two + 2], two[small_two + 3]]),
        two[small_two + 4 : small_two + 4 + table_rows].reshape(-1)[:table_size].reshape(
            grad_table.shape
        ),
        grad_out_w,
        one[s + 2],
        one[s],
        one[s + 1],
        grad_up_w,
        one[s + 4 : s + 4 + chunks].reshape(-1),
        grad_down_w,
        one[s + 3],
    )


def solution(mesh, interpret=False):
    sizes = dict(mesh.shape)
    canvas = P("batch", "rows", None, None)
    placed = (canvas, P("batch"), P("batch", None)) + (P(),) * 13 + (canvas,)

    def body(*args):
        return on_device(sizes, interpret, *args)

    return jax.shard_map(
        body,
        mesh=mesh,
        in_specs=placed,
        out_specs=(canvas, canvas) + (P(),) * 13,
        check_vma=False,
    )
```

time: 475 us -> 248 us (0.52)
  local copies, waits for them, and re-layouts: 160 us -> 16.4 us
  matrix products: 127 us -> 1.26 us
  Pallas kernels: 0 us -> 91.2 us
  blocking collectives: 46.1 us -> 0 us
  starting transfers between devices: 6.07 us -> 45.3 us
  other arithmetic: 41 us -> 17.6 us
  between operations: 15.3 us -> 1.79 us
    dot_general x20 -> x2, matrix products: 127 us -> 1.26 us  [the longest x1 0.88 us: on_device(): lax.dot_general(pair_offsets().astype(F32).reshape(-1, TOK * TOK), pairs_...]
    pallas_call x0 -> x2, Pallas kernels: none -> 91.2 us  [the longest x1 60.2 us: on_device(): pl.pallas_call(forward_kernel, grid=grid, in_specs=[in_smem(), in_smem(),...]
    psum x1 -> x0, waiting for transfers between devices: 75.1 us -> none  [on_device(): lax.psum((grad_pre_gain, grad_pre_shift, grad_in_w, grad_in_b, grad_table...]
    ppermute x2 -> x52, waiting for transfers between devices: 0.01 us -> 74.2 us  [the longest x50 74.2 us: swapped(): return lax.ppermute(value, axis, [(n, n ^ 1 << bit) for n in range(count)])]
    reshape x8, local copies, waits for them, and re-layouts: 64.3 us -> 2.71 us  [the longest x1 1.27 us: on_device(): pairs_grad = table.reshape(groups, PAD, GROUP, PAD)[:, :TOK, :, :TOK]]
    psum x1 -> x0, blocking collectives: 46.1 us -> none  [on_device(): lax.psum((grad_pre_gain, grad_pre_shift, grad_in_w, grad_in_b, grad_table...]
    ppermute x2 -> x52, starting transfers between devices: 6.04 us -> 45.3 us  [the longest x50 39.1 us: swapped(): return lax.ppermute(value, axis, [(n, n ^ 1 << bit) for n in range(count)])]
    convert_element_type x11 -> x25, local copies, waits for them, and re-layouts: 32.3 us -> 0.68 us  [halved(): sent = lax.dynamic_slice_in_dim(value, (1 - bit) * half, half).astype(BF16)]
  transfers between devices with their start and end apart: 3 -> 52, of which waited for: 1 -> 26; matrix products, arithmetic and copies ran while one was open for 14% -> 10% of each run, Pallas kernels for 0% -> 0%
where the time goes in v1:
time: 248 us
  Pallas kernels  91.2 us (37%)
  waiting for transfers between devices  74.2 us (30%)
  starting transfers between devices  45.3 us (18%)
  other arithmetic  17.6 us (7%)
  local copies, waits for them, and re-layouts  16.4 us (7%)
    ppermute x50, waiting for transfers between devices, swapped(): return lax.ppermute(value, axis, [(n, n ^ 1 << bit) for n in range(count)])  74.2 us
    pallas_call x1, Pallas kernels, on_device(): pl.pallas_call(forward_kernel, grid=grid, in_specs=[in_smem(), in_smem(),...  60.2 us
    ppermute x50, starting transfers between devices, swapped(): return lax.ppermute(value, axis, [(n, n ^ 1 << bit) for n in range(count)])  39.1 us
    pallas_call x1, Pallas kernels, on_device(): pl.pallas_call(backward_kernel, grid=grid, in_specs=[in_smem(), by_image(...  31.1 us
    ppermute x1, starting transfers between devices, on_device(): lax.ppermute(patches[:, :SHIFT].reshape(images, edge, channels), 'rows',...  6.09 us
    convert_element_type x6, other arithmetic, placements(): return ({k: v.astype(BF16) for k, v in mats.items()}, col[:, None])  5.03 us
  transfers between devices with their start and end apart: 52, of which 26 were waited for; matrix products, arithmetic and copies ran while one was open for 10% of the time, Pallas kernels for 0%

profile of v1, /device:TPU:0, one launch (start us, length us, event | category | flops | bytes accessed | tf_op | source)
XLA Modules:
  0.0 247.8 jit_solution(6339661622548587688)
XLA Ops:
  1.8 6.1 %collective-permute-start = (bf16[4,168,384]{2,1,0:T(8,128)(2,1)S(1)}, bf16[4,168,384]{2,1,0:T(8,128)(2,1)S(1)}, u32[]{:S(2)}, u32[]{:S(2)}) collective-permute-start(bf16[4,168,384]{2,1,0:T(8,128)(2,1)S(1)} %bitcast.28), channel_id=1, source_target_pairs={{0,28},{4,0},{8,4},{12,8},{16,12},{20,16},{24,20},{28,24},{1,29},{... | collective-permute-start | bytes 1548296 | tf_op jit(solution)/shard_map/ppermute | solution.py:497
  20.8 60.2 %forward_mlp.1 = (bf16[4,392,384]{2,1,0:T(8,128)(2,1)}, bf16[4,448,384]{2,1,0:T(8,128)(2,1)}, bf16[4,448,1152]{2,1,0:T(8,128)(2,1)}, bf16[4,4,3,112,224]{4,3,2,1...) custom-call(s32[4]{0:T(128)} %widths_ref.3, s32[4,2]{1,0:T(4,128)} %copy.36.keep_ref, ...), custom_call_target="tpu_custom_call" | custom-call | tf_op jit(solution)/shard_map/forward_mlp/pallas_call | solution.py:527
  81.0 31.1 %attention_back.1 = (f32[4,224,384]{2,1,0:T(8,128)}, bf16[4,168,384]{2,1,0:T(8,128)(2,1)}, f32[1280,384]{1,0:T(8,128)}, f32[3,56,224]{2,1,0:T(8,128)}) custom-call(s32[4]{0:T(128)} %widths_ref.3, bf16[4,448,384]{2,1,0:T(8,128)(2,1)} %get-tuple-element.27.xs_ref, bf16[4,448,1152]{2,1,0:T(8,128)(2,1)} %get-tuple-element.28.qkv_ref, ...), custom_call_target="tpu_custom_call" | custom-call | tf_op jit(solution)/shard_map/attention_back/pallas_call | solution.py:594
  115.0 2.4 fusion.40
  117.5 1.6 slice.108
  121.5 3.1 %collective-permute-done.3 = bf16[128,384]{1,0:T(8,128)(2,1)S(1)} collective-permute-done((bf16[128,384]{1,0:T(8,128)(2,1)S(1)}, bf16[128,384]{1,0:T(8,128)(2,1)S(1)}, u32[]{:S(2)}, u32[]{:S(2)}) %collective-permute-start.3) | collective-permute-done | bytes 98336 | tf_op jit(solution)/shard_map/ppermute | solution.py:426
  124.9 12.1 %collective-permute-done.4 = bf16[64,384]{1,0:T(8,128)(2,1)S(1)} collective-permute-done((bf16[64,384]{1,0:T(8,128)(2,1)S(1)}, bf16[64,384]{1,0:T(8,128)(2,1)S(1)}, u32[]{:S(2)}, u32[]{:S(2)}) %collective-permute-start.4) | collective-permute-done | bytes 49184 | tf_op jit(solution)/shard_map/ppermute | solution.py:426
  137.2 3.7 %collective-permute-done.5 = bf16[32,384]{1,0:T(8,128)(2,1)S(1)} collective-permute-done((bf16[32,384]{1,0:T(8,128)(2,1)S(1)}, bf16[32,384]{1,0:T(8,128)(2,1)S(1)}, u32[]{:S(2)}, u32[]{:S(2)}) %collective-permute-start.5) | collective-permute-done | bytes 24608 | tf_op jit(solution)/shard_map/ppermute | solution.py:426
  141.1 4.5 %collective-permute-done.6 = bf16[16,384]{1,0:T(8,128)(2,1)S(1)} collective-permute-done((bf16[16,384]{1,0:T(8,128)(2,1)S(1)}, bf16[16,384]{1,0:T(8,128)(2,1)S(1)}, u32[]{:S(2)}, u32[]{:S(2)}) %collective-permute-start.6) | collective-permute-done | bytes 12320 | tf_op jit(solution)/shard_map/ppermute | solution.py:426
  145.7 4.5 %collective-permute-done.7 = bf16[16,384]{1,0:T(8,128)(2,1)S(1)} collective-permute-done((bf16[16,384]{1,0:T(8,128)(2,1)S(1)}, bf16[16,384]{1,0:T(8,128)(2,1)S(1)}, u32[]{:S(2)}, u32[]{:S(2)}) %collective-permute-start.7) | collective-permute-done | bytes 12320 | tf_op jit(solution)/shard_map/ppermute | solution.py:426
  150.5 3.9 %collective-permute-done.8 = bf16[32,384]{1,0:T(8,128)(2,1)S(1)} collective-permute-done((bf16[32,384]{1,0:T(8,128)(2,1)S(1)}, bf16[32,384]{1,0:T(8,128)(2,1)S(1)}, u32[]{:S(2)}, u32[]{:S(2)}) %collective-permute-start.8) | collective-permute-done | bytes 24608 | tf_op jit(solution)/shard_map/ppermute | solution.py:426
  156.6 3.2 %collective-permute-done.9 = bf16[64,384]{1,0:T(8,128)(2,1)S(1)} collective-permute-done((bf16[64,384]{1,0:T(8,128)(2,1)S(1)}, bf16[64,384]{1,0:T(8,128)(2,1)S(1)}, u32[]{:S(2)}, u32[]{:S(2)}) %collective-permute-start.9) | collective-permute-done | bytes 49184 | tf_op jit(solution)/shard_map/ppermute | solution.py:426
  160.7 1.6 collective-permute-start.10
  162.5 2.5 %collective-permute-start.33 = (bf16[320,384]{1,0:T(8,128)(2,1)S(1)}, bf16[320,384]{1,0:T(8,128)(2,1)S(1)}, u32[]{:S(2)}, u32[]{:S(2)}) collective-permute-start(bf16[320,384]{1,0:T(8,128)(2,1)S(1)} %dynamic-slice_convert_fusion.4), channel_id=1, source_target_pairs={{0,4},{4,0},{8,12},{12,8},{16,20},{20,16},{24,28},{28,24},{1,5},{5... | collective-permute-start | bytes 737288 | tf_op jit(solution)/shard_map/ppermute | solution.py:426
  167.5 1.8 collective-permute-done.15
  170.0 1.6 pad_maximum_fusion
  171.6 2.4 collective-permute-done.16
  174.9 3.8 %collective-permute-done.17 = bf16[24,384]{1,0:T(8,128)(2,1)S(1)} collective-permute-done((bf16[24,384]{1,0:T(8,128)(2,1)S(1)}, bf16[24,384]{1,0:T(8,128)(2,1)S(1)}, u32[]{:S(2)}, u32[]{:S(2)}) %collective-permute-start.17) | collective-permute-done | bytes 18464 | tf_op jit(solution)/shard_map/ppermute | solution.py:426
  181.0 1.8 collective-permute-done.18
  182.9 1.7 collective-permute-done.44
  185.6 1.7 collective-permute-done.19
  190.4 4.2 %collective-permute-done.46 = bf16[32,384]{1,0:T(8,128)(2,1)S(1)} collective-permute-done((bf16[32,384]{1,0:T(8,128)(2,1)S(1)}, bf16[32,384]{1,0:T(8,128)(2,1)S(1)}, u32[]{:S(2)}, u32[]{:S(2)}) %collective-permute-start.46) | collective-permute-done | bytes 24608 | tf_op jit(solution)/shard_map/ppermute | solution.py:426
  196.6 2.8 %collective-permute-done.47 = bf16[32,384]{1,0:T(8,128)(2,1)S(1)} collective-permute-done((bf16[32,384]{1,0:T(8,128)(2,1)S(1)}, bf16[32,384]{1,0:T(8,128)(2,1)S(1)}, u32[]{:S(2)}, u32[]{:S(2)}) %collective-permute-start.47) | collective-permute-done | bytes 24608 | tf_op jit(solution)/shard_map/ppermute | solution.py:426
  200.1 3.4 %collective-permute-done.48 = bf16[64,384]{1,0:T(8,128)(2,1)S(1)} collective-permute-done((bf16[64,384]{1,0:T(8,128)(2,1)S(1)}, bf16[64,384]{1,0:T(8,128)(2,1)S(1)}, u32[]{:S(2)}, u32[]{:S(2)}) %collective-permute-start.48) | collective-permute-done | bytes 49184 | tf_op jit(solution)/shard_map/ppermute | solution.py:426
  203.6 1.9 collective-permute-start.49
  207.2 3.0 %collective-permute-done.35 = bf16[80,384]{1,0:T(8,128)(2,1)S(1)} collective-permute-done((bf16[80,384]{1,0:T(8,128)(2,1)S(1)}, bf16[80,384]{1,0:T(8,128)(2,1)S(1)}, u32[]{:S(2)}, u32[]{:S(2)}) %collective-permute-start.35) | collective-permute-done | bytes 61472 | tf_op jit(solution)/shard_map/ppermute | solution.py:426
  211.6 1.8 collective-permute-start.26
  216.5 2.0 collective-permute-start.27
  220.1 1.6 collective-permute-start.38
  227.4 2.0 collective-permute-done.39
  233.0 3.3 %collective-permute-done.40 = bf16[320,384]{1,0:T(8,128)(2,1)S(1)} collective-permute-done((bf16[320,384]{1,0:T(8,128)(2,1)S(1)}, bf16[320,384]{1,0:T(8,128)(2,1)S(1)}, u32[]{:S(2)}, u32[]{:S(2)}) %collective-permute-start.40) | collective-permute-done | bytes 245792 | tf_op jit(solution)/shard_map/ppermute | solution.py:426
  246.0 1.7 pad_maximum_fusion.1
  (260 shorter events, 62.7 us)
Async XLA Ops:
  1.8 18.2 %collective-permute-start = (bf16[4,168,384]{2,1,0:T(8,128)(2,1)S(1)}, bf16[4,168,384]{2,1,0:T(8,128)(2,1)S(1)}, u32[]{:S(2)}, u32[]{:S(2)}) collective-permute-start(bf16[4,168,384]{2,1,0:T(8,128)(2,1)S(1)} %bitcast.28), channel_id=1, source_target_pairs={{0,28},{4,0},{8,4},{12,8},{16,12},{20,16},{24,20},{28,24},{1,29},{... | collective-permute-start | bytes 1548296 | tf_op jit(solution)/shard_map/ppermute | solution.py:497
  114.9 4.8 %collective-permute-start.2 = (bf16[256,384]{1,0:T(8,128)(2,1)S(1)}, bf16[256,384]{1,0:T(8,128)(2,1)S(1)}, u32[]{:S(2)}, u32[]{:S(2)}) collective-permute-start(bf16[256,384]{1,0:T(8,128)(2,1)S(1)} %dynamic-slice_convert_fusion.7), channel_id=1, source_target_pairs={{0,1},{1,0},{2,3},{3,2},{4,5},{5,4},{6,7},{7,6},{8,9},{9,8},{10,11... | collective-permute-start | bytes 589832 | tf_op jit(solution)/shard_map/ppermute | solution.py:426
  119.0 47.3 %collective-permute-start.1 = (bf16[4,168,384]{2,1,0:T(8,128)(2,1)S(1)}, bf16[4,168,384]{2,1,0:T(8,128)(2,1)S(1)}, u32[]{:S(2)}, u32[]{:S(2)}) collective-permute-start(bf16[4,168,384]{2,1,0:T(8,128)(2,1)S(1)} %copy-done.14), channel_id=1, source_target_pairs={{0,4},{4,8},{8,12},{12,16},{16,20},{20,24},{24,28},{28,0},{1,5},{5... | collective-permute-start | bytes 1548296 | tf_op jit(solution)/shard_map/ppermute | solution.py:639
  119.2 21.8 %collective-permute-start.12 = (bf16[384,384]{1,0:T(8,128)(2,1)S(1)}, bf16[384,384]{1,0:T(8,128)(2,1)S(1)}, u32[]{:S(2)}, u32[]{:S(2)}) collective-permute-start(bf16[384,384]{1,0:T(8,128)(2,1)S(1)} %dynamic-slice_convert_fusion.3), channel_id=1, source_target_pairs={{0,1},{1,0},{2,3},{3,2},{4,5},{5,4},{6,7},{7,6},{8,9},{9,8},{10,11... | collective-permute-start | bytes 884744 | tf_op jit(solution)/shard_map/ppermute | solution.py:426
  121.4 28.9 %collective-permute-start.42 = (bf16[512,384]{1,0:T(8,128)(2,1)S(1)}, bf16[512,384]{1,0:T(8,128)(2,1)S(1)}, u32[]{:S(2)}, u32[]{:S(2)}) collective-permute-start(bf16[512,384]{1,0:T(8,128)(2,1)S(1)} %dynamic-slice_convert_fusion.2), channel_id=1, source_target_pairs={{0,1},{1,0},{2,3},{3,2},{4,5},{5,4},{6,7},{7,6},{8,9},{9,8},{10,11... | collective-permute-start | bytes 1179656 | tf_op jit(solution)/shard_map/ppermute | solution.py:426
  124.6 12.3 %collective-permute-start.4 = (bf16[64,384]{1,0:T(8,128)(2,1)S(1)}, bf16[64,384]{1,0:T(8,128)(2,1)S(1)}, u32[]{:S(2)}, u32[]{:S(2)}) collective-permute-start(bf16[64,384]{1,0:T(8,128)(2,1)S(1)} %dynamic-slice_convert_fusion.17), channel_id=1, source_target_pairs={{0,4},{4,0},{8,12},{12,8},{16,20},{20,16},{24,28},{28,24},{1,5},{5... | collective-permute-start | bytes 147464 | tf_op jit(solution)/shard_map/ppermute | solution.py:426
  124.8 35.9 %collective-permute-start.32 = (bf16[640,384]{1,0:T(8,128)(2,1)S(1)}, bf16[640,384]{1,0:T(8,128)(2,1)S(1)}, u32[]{:S(2)}, u32[]{:S(2)}) collective-permute-start(bf16[640,384]{1,0:T(8,128)(2,1)S(1)} %dynamic-slice_convert_fusion), channel_id=1, source_target_pairs={{0,1},{1,0},{2,3},{3,2},{4,5},{5,4},{6,7},{7,6},{8,9},{9,8},{10,11... | collective-permute-start | bytes 1474568 | tf_op jit(solution)/shard_map/ppermute | solution.py:426
  140.9 21.6 %collective-permute-start.22 = (bf16[640,384]{1,0:T(8,128)(2,1)S(1)}, bf16[640,384]{1,0:T(8,128)(2,1)S(1)}, u32[]{:S(2)}, u32[]{:S(2)}) collective-permute-start(bf16[640,384]{1,0:T(8,128)(2,1)S(1)} %dynamic-slice_convert_fusion.1), channel_id=1, source_target_pairs={{0,1},{1,0},{2,3},{3,2},{4,5},{5,4},{6,7},{7,6},{8,9},{9,8},{10,11... | collective-permute-start | bytes 1474568 | tf_op jit(solution)/shard_map/ppermute | solution.py:426
  150.3 5.5 %collective-permute-start.13 = (bf16[192,384]{1,0:T(8,128)(2,1)S(1)}, bf16[192,384]{1,0:T(8,128)(2,1)S(1)}, u32[]{:S(2)}, u32[]{:S(2)}) collective-permute-start(bf16[192,384]{1,0:T(8,128)(2,1)S(1)} %dynamic-slice_convert_fusion.8), channel_id=1, source_target_pairs={{0,4},{4,0},{8,12},{12,8},{16,20},{20,16},{24,28},{28,24},{1,5},{5... | collective-permute-start | bytes 442376 | tf_op jit(solution)/shard_map/ppermute | solution.py:426
  154.5 25.4 %collective-permute-start.43 = (bf16[256,384]{1,0:T(8,128)(2,1)S(1)}, bf16[256,384]{1,0:T(8,128)(2,1)S(1)}, u32[]{:S(2)}, u32[]{:S(2)}) collective-permute-start(bf16[256,384]{1,0:T(8,128)(2,1)S(1)} %dynamic-slice_convert_fusion.6), channel_id=1, source_target_pairs={{0,8},{4,12},{8,0},{12,4},{16,24},{20,28},{24,16},{28,20},{1,9},{5... | collective-permute-start | bytes 589832 | tf_op jit(solution)/shard_map/ppermute | solution.py:426
  159.8 5.3 %collective-permute-start.14 = (bf16[96,384]{1,0:T(8,128)(2,1)S(1)}, bf16[96,384]{1,0:T(8,128)(2,1)S(1)}, u32[]{:S(2)}, u32[]{:S(2)}) collective-permute-start(bf16[96,384]{1,0:T(8,128)(2,1)S(1)} %dynamic-slice_convert_fusion.13), channel_id=1, source_target_pairs={{0,8},{4,12},{8,0},{12,4},{16,24},{20,28},{24,16},{28,20},{1,9},{5... | collective-permute-start | bytes 221192 | tf_op jit(solution)/shard_map/ppermute | solution.py:426
  160.7 14.1 %collective-permute-start.10 = (bf16[128,384]{1,0:T(8,128)(2,1)S(1)}, bf16[128,384]{1,0:T(8,128)(2,1)S(1)}, u32[]{:S(2)}, u32[]{:S(2)}) collective-permute-start(bf16[128,384]{1,0:T(8,128)(2,1)S(1)} %maximum_select_fusion.16), channel_id=1, source_target_pairs={{0,2},{1,3},{2,0},{3,1},{4,6},{5,7},{6,4},{7,5},{8,10},{9,11},{10,... | collective-permute-start | bytes 294920 | tf_op jit(solution)/shard_map/ppermute | solution.py:426
  162.5 26.2 %collective-permute-start.33 = (bf16[320,384]{1,0:T(8,128)(2,1)S(1)}, bf16[320,384]{1,0:T(8,128)(2,1)S(1)}, u32[]{:S(2)}, u32[]{:S(2)}) collective-permute-start(bf16[320,384]{1,0:T(8,128)(2,1)S(1)} %dynamic-slice_convert_fusion.4), channel_id=1, source_target_pairs={{0,4},{4,0},{8,12},{12,8},{16,20},{20,16},{24,28},{28,24},{1,5},{5... | collective-permute-start | bytes 737288 | tf_op jit(solution)/shard_map/ppermute | solution.py:426
  166.3 24.0 %collective-permute-start.23 = (bf16[320,384]{1,0:T(8,128)(2,1)S(1)}, bf16[320,384]{1,0:T(8,128)(2,1)S(1)}, u32[]{:S(2)}, u32[]{:S(2)}) collective-permute-start(bf16[320,384]{1,0:T(8,128)(2,1)S(1)} %dynamic-slice_convert_fusion.5), channel_id=1, source_target_pairs={{0,2},{1,3},{2,0},{3,1},{4,6},{5,7},{6,4},{7,5},{8,10},{9,11},{10,... | collective-permute-start | bytes 737288 | tf_op jit(solution)/shard_map/ppermute | solution.py:426
  174.8 25.2 %collective-permute-start.11 = (bf16[256,384]{1,0:T(8,128)(2,1)S(1)}, bf16[256,384]{1,0:T(8,128)(2,1)S(1)}, u32[]{:S(2)}, u32[]{:S(2)}) collective-permute-start(bf16[256,384]{1,0:T(8,128)(2,1)S(1)} %maximum_select_fusion.11), channel_id=1, source_target_pairs={{0,1},{1,0},{2,3},{3,2},{4,5},{5,4},{6,7},{7,6},{8,9},{9,8},{10,11... | collective-permute-start | bytes 589832 | tf_op jit(solution)/shard_map/ppermute | solution.py:426
  184.7 5.1 %collective-permute-start.45 = (bf16[64,384]{1,0:T(8,128)(2,1)S(1)}, bf16[64,384]{1,0:T(8,128)(2,1)S(1)}, u32[]{:S(2)}, u32[]{:S(2)}) collective-permute-start(bf16[64,384]{1,0:T(8,128)(2,1)S(1)} %dynamic-slice_convert_fusion.16), channel_id=1, source_target_pairs={{0,4},{4,0},{8,12},{12,8},{16,20},{20,16},{24,28},{28,24},{1,5},{5... | collective-permute-start | bytes 147464 | tf_op jit(solution)/shard_map/ppermute | solution.py:426
  187.2 18.3 %collective-permute-start.20 = (bf16[192,384]{1,0:T(8,128)(2,1)S(1)}, bf16[192,384]{1,0:T(8,128)(2,1)S(1)}, u32[]{:S(2)}, u32[]{:S(2)}) collective-permute-start(bf16[192,384]{1,0:T(8,128)(2,1)S(1)} %maximum_select_fusion.13), channel_id=1, source_target_pairs={{0,4},{4,0},{8,12},{12,8},{16,20},{20,16},{24,28},{28,24},{1,5},{5... | collective-permute-start | bytes 442376 | tf_op jit(solution)/shard_map/ppermute | solution.py:426
  188.7 17.0 %collective-permute-start.34 = (bf16[160,384]{1,0:T(8,128)(2,1)S(1)}, bf16[160,384]{1,0:T(8,128)(2,1)S(1)}, u32[]{:S(2)}, u32[]{:S(2)}) collective-permute-start(bf16[160,384]{1,0:T(8,128)(2,1)S(1)} %dynamic-slice_convert_fusion.9), channel_id=1, source_target_pairs={{0,8},{4,12},{8,0},{12,4},{16,24},{20,28},{24,16},{28,20},{1,9},{5... | collective-permute-start | bytes 368648 | tf_op jit(solution)/shard_map/ppermute | solution.py:426
  195.9 10.1 %collective-permute-start.24 = (bf16[160,384]{1,0:T(8,128)(2,1)S(1)}, bf16[160,384]{1,0:T(8,128)(2,1)S(1)}, u32[]{:S(2)}, u32[]{:S(2)}) collective-permute-start(bf16[160,384]{1,0:T(8,128)(2,1)S(1)} %dynamic-slice_convert_fusion.10), channel_id=1, source_target_pairs={{0,4},{4,0},{8,12},{12,8},{16,20},{20,16},{24,28},{28,24},{1,5},{5... | collective-permute-start | bytes 368648 | tf_op jit(solution)/shard_map/ppermute | solution.py:426
  203.6 9.8 %collective-permute-start.49 = (bf16[128,384]{1,0:T(8,128)(2,1)S(1)}, bf16[128,384]{1,0:T(8,128)(2,1)S(1)}, u32[]{:S(2)}, u32[]{:S(2)}) collective-permute-start(bf16[128,384]{1,0:T(8,128)(2,1)S(1)} %maximum_select_fusion.17), channel_id=1, source_target_pairs={{0,2},{1,3},{2,0},{3,1},{4,6},{5,7},{6,4},{7,5},{8,10},{9,11},{10,... | collective-permute-start | bytes 294920 | tf_op jit(solution)/shard_map/ppermute | solution.py:426
  205.6 21.5 %collective-permute-start.21 = (bf16[384,384]{1,0:T(8,128)(2,1)S(1)}, bf16[384,384]{1,0:T(8,128)(2,1)S(1)}, u32[]{:S(2)}, u32[]{:S(2)}) collective-permute-start(bf16[384,384]{1,0:T(8,128)(2,1)S(1)} %maximum_select_fusion.8), channel_id=1, source_target_pairs={{0,1},{1,0},{2,3},{3,2},{4,5},{5,4},{6,7},{7,6},{8,9},{9,8},{10,11... | collective-permute-start | bytes 884744 | tf_op jit(solution)/shard_map/ppermute | solution.py:426
  206.1 5.5 %collective-permute-start.25 = (bf16[80,384]{1,0:T(8,128)(2,1)S(1)}, bf16[80,384]{1,0:T(8,128)(2,1)S(1)}, u32[]{:S(2)}, u32[]{:S(2)}) collective-permute-start(bf16[80,384]{1,0:T(8,128)(2,1)S(1)} %dynamic-slice_convert_fusion.15), channel_id=1, source_target_pairs={{0,8},{4,12},{8,0},{12,4},{16,24},{20,28},{24,16},{28,20},{1,9},{5... | collective-permute-start | bytes 184328 | tf_op jit(solution)/shard_map/ppermute | solution.py:426
  210.3 4.9 %collective-permute-start.36 = (bf16[40,384]{1,0:T(8,128)(2,1)S(1)}, bf16[40,384]{1,0:T(8,128)(2,1)S(1)}, u32[]{:S(2)}, u32[]{:S(2)}) collective-permute-start(bf16[40,384]{1,0:T(8,128)(2,1)S(1)} %dynamic-slice_convert_fusion.19), channel_id=1, source_target_pairs={{0,16},{4,20},{8,24},{12,28},{16,0},{20,4},{24,8},{28,12},{1,17},{... | collective-permute-start | bytes 92168 | tf_op jit(solution)/shard_map/ppermute | solution.py:426
  211.6 5.0 %collective-permute-start.26 = (bf16[40,384]{1,0:T(8,128)(2,1)S(1)}, bf16[40,384]{1,0:T(8,128)(2,1)S(1)}, u32[]{:S(2)}, u32[]{:S(2)}) collective-permute-start(bf16[40,384]{1,0:T(8,128)(2,1)S(1)} %dynamic-slice_convert_fusion.20), channel_id=1, source_target_pairs={{0,16},{4,20},{8,24},{12,28},{16,0},{20,4},{24,8},{28,12},{1,17},{... | collective-permute-start | bytes 92168 | tf_op jit(solution)/shard_map/ppermute | solution.py:426
  213.4 13.4 %collective-permute-start.50 = (bf16[256,384]{1,0:T(8,128)(2,1)S(1)}, bf16[256,384]{1,0:T(8,128)(2,1)S(1)}, u32[]{:S(2)}, u32[]{:S(2)}) collective-permute-start(bf16[256,384]{1,0:T(8,128)(2,1)S(1)} %maximum_select_fusion.12), channel_id=1, source_target_pairs={{0,8},{4,12},{8,0},{12,4},{16,24},{20,28},{24,16},{28,20},{1,9},{5... | collective-permute-start | bytes 589832 | tf_op jit(solution)/shard_map/ppermute | solution.py:426
  215.2 5.0 %collective-permute-start.37 = (bf16[40,384]{1,0:T(8,128)(2,1)S(1)}, bf16[40,384]{1,0:T(8,128)(2,1)S(1)}, u32[]{:S(2)}, u32[]{:S(2)}) collective-permute-start(bf16[40,384]{1,0:T(8,128)(2,1)S(1)} %add_convert_fusion), channel_id=1, source_target_pairs={{0,16},{4,20},{8,24},{12,28},{16,0},{20,4},{24,8},{28,12},{1,17},{... | collective-permute-start | bytes 92168 | tf_op jit(solution)/shard_map/ppermute | solution.py:426
  216.5 5.2 %collective-permute-start.27 = (bf16[40,384]{1,0:T(8,128)(2,1)S(1)}, bf16[40,384]{1,0:T(8,128)(2,1)S(1)}, u32[]{:S(2)}, u32[]{:S(2)}) collective-permute-start(bf16[40,384]{1,0:T(8,128)(2,1)S(1)} %add_convert_fusion.1), channel_id=1, source_target_pairs={{0,16},{4,20},{8,24},{12,28},{16,0},{20,4},{24,8},{28,12},{1,17},{... | collective-permute-start | bytes 92168 | tf_op jit(solution)/shard_map/ppermute | solution.py:426
  224.5 4.9 %collective-permute-start.39 = (bf16[160,384]{1,0:T(8,128)(2,1)S(1)}, bf16[160,384]{1,0:T(8,128)(2,1)S(1)}, u32[]{:S(2)}, u32[]{:S(2)}) collective-permute-start(bf16[160,384]{1,0:T(8,128)(2,1)S(1)} %maximum_select_fusion.15), channel_id=1, source_target_pairs={{0,8},{4,12},{8,0},{12,4},{16,24},{20,28},{24,16},{28,20},{1,9},{5... | collective-permute-start | bytes 368648 | tf_op jit(solution)/shard_map/ppermute | solution.py:426
  226.1 5.3 %collective-permute-start.29 = (bf16[160,384]{1,0:T(8,128)(2,1)S(1)}, bf16[160,384]{1,0:T(8,128)(2,1)S(1)}, u32[]{:S(2)}, u32[]{:S(2)}) collective-permute-start(bf16[160,384]{1,0:T(8,128)(2,1)S(1)} %maximum_select_fusion.14), channel_id=1, source_target_pairs={{0,4},{4,0},{8,12},{12,8},{16,20},{20,16},{24,28},{28,24},{1,5},{5... | collective-permute-start | bytes 368648 | tf_op jit(solution)/shard_map/ppermute | solution.py:426
  227.0 13.7 %collective-permute-start.51 = (bf16[512,384]{1,0:T(8,128)(2,1)S(1)}, bf16[512,384]{1,0:T(8,128)(2,1)S(1)}, u32[]{:S(2)}, u32[]{:S(2)}) collective-permute-start(bf16[512,384]{1,0:T(8,128)(2,1)S(1)} %maximum_select_fusion.7), channel_id=1, source_target_pairs={{0,1},{1,0},{2,3},{3,2},{4,5},{5,4},{6,7},{7,6},{8,9},{9,8},{10,11... | collective-permute-start | bytes 1179656 | tf_op jit(solution)/shard_map/ppermute | solution.py:426
  229.5 6.8 %collective-permute-start.40 = (bf16[320,384]{1,0:T(8,128)(2,1)S(1)}, bf16[320,384]{1,0:T(8,128)(2,1)S(1)}, u32[]{:S(2)}, u32[]{:S(2)}) collective-permute-start(bf16[320,384]{1,0:T(8,128)(2,1)S(1)} %maximum_select_fusion.10), channel_id=1, source_target_pairs={{0,4},{4,0},{8,12},{12,8},{16,20},{20,16},{24,28},{28,24},{1,5},{5... | collective-permute-start | bytes 737288 | tf_op jit(solution)/shard_map/ppermute | solution.py:426
  231.5 7.8 %collective-permute-start.30 = (bf16[320,384]{1,0:T(8,128)(2,1)S(1)}, bf16[320,384]{1,0:T(8,128)(2,1)S(1)}, u32[]{:S(2)}, u32[]{:S(2)}) collective-permute-start(bf16[320,384]{1,0:T(8,128)(2,1)S(1)} %maximum_select_fusion.9), channel_id=1, source_target_pairs={{0,2},{1,3},{2,0},{3,1},{4,6},{5,7},{6,4},{7,5},{8,10},{9,11},{10,... | collective-permute-start | bytes 737288 | tf_op jit(solution)/shard_map/ppermute | solution.py:426
  (35 other events, 139.1 us)

commit v2 on v1

--- a/solution.py
+++ b/solution.py
@@ -242,7 +242,6 @@
     grad_own_ref,
     grad_halo_ref,
     acc_ref,
-    table_ref,
     proj_sc,
 ):
     i = pl.program_id(0)
@@ -254,7 +253,6 @@
     @pl.when(i == 0)
     def _():
         acc_ref[...] = jnp.zeros_like(acc_ref)
-        table_ref[...] = jnp.zeros_like(table_ref)
 
     def vec(n):
         return vec_ref[n : n + 1, :]
@@ -285,7 +283,8 @@
             for lo in (0, PAD):
                 side = weighted[lo : lo + PAD]
                 scores.append(side - probs[lo : lo + PAD] * col_sum(side))
-            table_ref[g] += scores[0] + scores[1]
+            first = 3 * channels + 8 + g * PAD
+            acc_ref[first : first + PAD, : GROUP * PAD] += scores[0] + scores[1]
             grad_s = jnp.concatenate(scores, axis=0).astype(BF16)
             grad_k = undiagonal(nn(grad_s, q)) * factor
             grad_q = unstacked(tn(grad_s, k), masks) * factor
@@ -411,57 +410,61 @@
     return bits
 
 
-def stage_orders(sizes):
-    first = [("batch", 0)]
-    rows = [("rows", b) for b in range(power_bits(sizes["rows"]))]
-    batch = [("batch", b) for b in range(1, power_bits(sizes["batch"]))]
+def chip_orders(sizes):
+    low = power_bits(sizes["batch"])
+    rows = [low + b for b in range(power_bits(sizes["rows"]))]
+    batch = list(range(1, low))
     lead = batch[:1] + rows[:2]
     rest = rows[2:] + batch[1:]
-    orders = [lead[k:] + lead[:k] + rest for k in range(len(lead))]
-    return first, orders
-
-
-def swapped(value, axis, bit):
-    count = lax.axis_size(axis)
-    return lax.ppermute(value, axis, [(n, n ^ (1 << bit)) for n in range(count)])
-
-
-def my_bit(axis, bit):
-    return (lax.axis_index(axis) >> bit) & 1
-
-
-def halved(value, stage):
+    return [lead + rest, lead[-1:] + lead[:-1] + rest]
+
+
+def swapped(value, bits):
+    total = lax.axis_size("rows") * lax.axis_size("batch")
+    pairs = [(n, n ^ (1 << bits[n & 1])) for n in range(total)]
+    return lax.ppermute(value, ("rows", "batch"), pairs)
+
+
+def my_bit(bits):
+    index = lax.axis_index("rows") * lax.axis_size("batch") + lax.axis_index("batch")
+    return jnp.where(index & 1 == 0, index >> bits[0], index >> bits[1]) & 1
+
+
+def halves(value, bit):
     half = value.shape[0] // 2
-    bit = my_bit(*stage)
-    sent = lax.dynamic_slice_in_dim(value, (1 - bit) * half, half).astype(BF16)
-    keep = lax.dynamic_slice_in_dim(value, bit * half, half)
-    return keep + swapped(sent, *stage).astype(F32)
-
-
-def doubled(value, stage):
-    other = swapped(value, *stage)
-    bit = my_bit(*stage)
+    return (
+        lax.dynamic_slice_in_dim(value, bit * half, half),
+        lax.dynamic_slice_in_dim(value, (1 - bit) * half, half),
+    )
+
+
+def ordered(bit, mine, other):
     return jnp.where(
-        bit == 0, jnp.concatenate([value, other]), jnp.concatenate([other, value])
-    )
-
-
-def summed_over_devices(value, cuts, sizes):
-    first, orders = stage_orders(sizes)
-    parts, start = [], 0
-    for rows in cuts:
-        parts.append(value[start : start + rows])
-        start += rows
-    for stage in first:
-        parts = [halved(p, stage) for p in parts]
-    for step in range(len(orders[0])):
-        parts = [halved(p, orders[n % len(orders)][step]) for n, p in enumerate(parts)]
-    parts = [p.astype(BF16) for p in parts]
-    for step in reversed(range(len(orders[0]))):
-        parts = [doubled(p, orders[n % len(orders)][step]) for n, p in enumerate(parts)]
-    for stage in first:
-        parts = [doubled(p, stage) for p in parts]
-    return parts
+        bit == 0, jnp.concatenate([mine, other]), jnp.concatenate([other, mine])
+    )
+
+
+def summed_over_devices(values, sizes):
+    core = (0, 0)
+    steps = list(zip(*chip_orders(sizes)))
+    bit = my_bit(core)
+    split = [halves(v, bit) for v in values]
+    sent = jnp.concatenate([away.astype(BF16) for _, away in split])
+    kept_rows = jnp.concatenate([keep for keep, _ in split])
+    part = kept_rows + swapped(sent, core).astype(F32)
+    for bits in steps:
+        keep, away = halves(part, my_bit(bits))
+        part = keep + swapped(away.astype(BF16), bits).astype(F32)
+    part = part.astype(BF16)
+    for bits in reversed(steps):
+        part = ordered(my_bit(bits), part, swapped(part, bits))
+    other = swapped(part, core)
+    sums, start = [], 0
+    for v in values:
+        rows = slice(start, start + v.shape[0] // 2)
+        sums.append(ordered(bit, part[rows], other[rows]))
+        start = rows.stop
+    return sums
 
 
 def on_device(sizes, interpret, *args):
@@ -522,8 +525,8 @@
     params = pltpu.CompilerParams(
         dimension_semantics=("arbitrary",), vmem_limit_bytes=60 * 1024 * 1024
     )
-    rows_one = 2 * hidden + channels + 128
-    rows_two = 3 * channels + 128
+    rows_one = 2 * hidden + channels + 64
+    rows_two = 3 * channels + 192
     output, xs, qkv, probs, grad_after, grad_mixed, acc_one = pl.pallas_call(
         forward_kernel,
         grid=grid,
@@ -591,7 +594,7 @@
         up_weight,
         down_weight,
     )
-    grad_own, grad_halo, acc_two, table = pl.pallas_call(
+    grad_own, grad_halo, acc_two = pl.pallas_call(
         backward_kernel,
         grid=grid,
         in_specs=[
@@ -611,13 +614,11 @@
             by_image((area - edge, channels)),
             by_image((edge, channels)),
             kept((rows_two, channels)),
-            kept((groups, PAD, GROUP * PAD)),
         ],
         out_shape=[
             jax.ShapeDtypeStruct((images, area - edge, channels), F32),
             jax.ShapeDtypeStruct((images, edge, channels), BF16),
             jax.ShapeDtypeStruct((rows_two, channels), F32),
-            jax.ShapeDtypeStruct((groups, PAD, GROUP * PAD), F32),
         ],
         scratch_shapes=[pltpu.VMEM((padded, 3 * channels), BF16)],
         compiler_params=params,
@@ -640,23 +641,19 @@
     grad_patches = jnp.concatenate([received.astype(F32), grad_own], axis=1).reshape(
         images, height, columns, channels
     )
-    pairs_grad = table.reshape(groups, PAD, GROUP, PAD)[:, :TOK, :, :TOK]
-    pairs_grad = pairs_grad.transpose(0, 2, 1, 3).reshape(HEADS, TOK * TOK)
+    small_two = 3 * channels
+    one, two = summed_over_devices((acc_one, acc_two), sizes)
+    table = two[small_two + 8 : small_two + 8 + groups * PAD, : GROUP * PAD]
+    table = table.reshape(groups, PAD, GROUP, PAD)[:, :TOK, :, :TOK]
+    table = table.transpose(0, 2, 1, 3).reshape(HEADS, TOK * TOK)
     grad_table = lax.dot_general(
-        pair_offsets().astype(F32).reshape(-1, TOK * TOK),
-        pairs_grad,
+        pair_offsets().astype(BF16).reshape(-1, TOK * TOK),
+        table,
         (((1,), (1,)), ((), ())),
-        precision=lax.Precision.HIGHEST,
         preferred_element_type=F32,
     )
-    table_size = grad_table.size
-    table_rows = -(-table_size // channels)
-    flat = jnp.pad(grad_table.reshape(-1), (0, table_rows * channels - table_size))
-    small_two = 3 * channels
-    acc_two = lax.dynamic_update_slice(acc_two, flat.reshape(table_rows, channels), (small_two + 4, 0))
-
-    one = jnp.concatenate(summed_over_devices(acc_one, (1280, 1280, 1024), sizes)).astype(F32)
-    two = jnp.concatenate(summed_over_devices(acc_two, (512, 768), sizes)).astype(F32)
+    one = one.astype(F32)
+    two = two.astype(F32)
     grad_down_w = one[:hidden]
     grad_up_w = jnp.concatenate(
         [one[hidden + c * channels : hidden + (c + 1) * channels] for c in range(chunks)], axis=1
@@ -673,9 +670,7 @@
         two[small_two + 1],
         grad_in_w,
         jnp.concatenate([two[small_two + 2], two[small_two + 3]]),
-        two[small_two + 4 : small_two + 4 + table_rows].reshape(-1)[:table_size].reshape(
-            grad_table.shape
-        ),
+        grad_table,
         grad_out_w,
         one[s + 2],
         one[s],

time: 248 us -> 244 us (0.984)
  starting transfers between devices: 45.3 us -> 10.3 us
  local copies, waits for them, and re-layouts: 16.4 us -> 29.7 us
  waiting for transfers between devices: 74.2 us -> 84.5 us
  other arithmetic: 17.6 us -> 23.7 us
    ppermute x50 -> x10, starting transfers between devices: 39.1 us -> 4.17 us  [swapped(): return lax.ppermute(value, ('rows', 'batch'), pairs)]
    ppermute x1, waiting for transfers between devices: 0.01 us -> 16.8 us  [on_device(): lax.ppermute(grad_halo, 'rows', [(n, (n + 1) % count) for n in range(coun...]
    ppermute x50 -> x10, waiting for transfers between devices: 74.2 us -> 67.8 us  [swapped(): return lax.ppermute(value, ('rows', 'batch'), pairs)]
    dynamic_slice x0 -> x2, local copies, waits for them, and re-layouts: none -> 3.24 us  [halves(): lax.dynamic_slice_in_dim(value, bit * half, half)]
    add x20 -> x4, other arithmetic: 0.73 us -> 3.66 us  [the longest x3 1.84 us: summed_over_devices(): part = keep + swapped(away.astype(BF16), bits).astype(F32)]
    convert_element_type x25 -> x6, local copies, waits for them, and re-layouts: 0.68 us -> 3.42 us  [the longest x2 3.19 us: summed_over_devices(): sent = jnp.concatenate([away.astype(BF16) for _, away in split])]
    slice x8 -> x10, local copies, waits for them, and re-layouts: 5.1 us -> 7.43 us  [the longest x4 2.75 us: summed_over_devices(): sums.append(ordered(bit, part[rows], other[rows]))]
  transfers between devices with their start and end apart: 52 -> 12, of which waited for: 26 -> 10; matrix products, arithmetic and copies ran while one was open for 10% -> 7% of each run, Pallas kernels for 0% -> 0%
where the time goes in v2:
time: 244 us; the launch traced here: 243 us
  Pallas kernels  91.2 us (37%)
  waiting for transfers between devices  84.5 us (35%)
  local copies, waits for them, and re-layouts  29.7 us (12%)
  other arithmetic  23.7 us (10%)
  starting transfers between devices  10.3 us (4%)
    ppermute x10, waiting for transfers between devices, swapped(): return lax.ppermute(value, ('rows', 'batch'), pairs)  67.8 us
    pallas_call x1, Pallas kernels, on_device(): pl.pallas_call(forward_kernel, grid=grid, in_specs=[in_smem(), in_smem(),...  60.1 us
    pallas_call x1, Pallas kernels, on_device(): pl.pallas_call(backward_kernel, grid=grid, in_specs=[in_smem(), by_image(...  31.1 us
    ppermute x1, waiting for transfers between devices, on_device(): lax.ppermute(grad_halo, 'rows', [(n, (n + 1) % count) for n in range(coun...  16.8 us
    ppermute x1, starting transfers between devices, on_device(): lax.ppermute(patches[:, :SHIFT].reshape(images, edge, channels), 'rows',...  6.09 us
    convert_element_type x6, other arithmetic, placements(): return ({k: v.astype(BF16) for k, v in mats.items()}, col[:, None])  4.98 us
  transfers between devices with their start and end apart: 12, of which 10 were waited for; matrix products, arithmetic and copies ran while one was open for 7% of the time, Pallas kernels for 0%

profile of v2, /device:TPU:0, one launch (start us, length us, event | category | flops | bytes accessed | tf_op | source)
XLA Modules:
  0.0 243.0 jit_solution(3976823990822614904)
XLA Ops:
  1.8 6.1 %collective-permute-start = (bf16[4,168,384]{2,1,0:T(8,128)(2,1)S(1)}, bf16[4,168,384]{2,1,0:T(8,128)(2,1)S(1)}, u32[]{:S(2)}, u32[]{:S(2)}) collective-permute-start(bf16[4,168,384]{2,1,0:T(8,128)(2,1)S(1)} %bitcast.28), channel_id=1, source_target_pairs={{0,28},{4,0},{8,4},{12,8},{16,12},{20,16},{24,20},{28,24},{1,29},{... | collective-permute-start | bytes 1548296 | tf_op jit(solution)/shard_map/ppermute | solution.py:500
  21.4 60.1 %forward_mlp.1 = (bf16[4,392,384]{2,1,0:T(8,128)(2,1)}, bf16[4,448,384]{2,1,0:T(8,128)(2,1)}, bf16[4,448,1152]{2,1,0:T(8,128)(2,1)}, bf16[4,4,3,112,224]{4,3,2,1...) custom-call(s32[4]{0:T(128)} %widths_ref.3, s32[4,2]{1,0:T(4,128)} %copy.35.keep_ref, ...), custom_call_target="tpu_custom_call" | custom-call | tf_op jit(solution)/shard_map/forward_mlp/pallas_call | solution.py:530
  81.5 31.1 %attention_back.1 = (f32[4,224,384]{2,1,0:T(8,128)}, bf16[4,168,384]{2,1,0:T(8,128)(2,1)}, f32[1344,384]{1,0:T(8,128)}) custom-call(s32[4]{0:T(128)} %widths_ref.3, bf16[4,448,384]{2,1,0:T(8,128)(2,1)} %get-tuple-element.26.xs_ref, bf16[4,448,1152]{2,1,0:T(8,128)(2,1)} %get-tuple-element.27.qkv_ref, bf16[4,4,3,112,224]{4,3,2,1,0:T(8,128)(2,1)} %get-tuple-element.28.prob_ref, ...), custom_call_target="tpu_custom_call" | custom-call | tf_op jit(solution)/shard_map/attention_back/pallas_call | solution.py:597
  112.6 1.3 dynamic-slice_convert_fusion.2
  113.9 1.9 dynamic-slice_convert_fusion
  116.1 1.3 constant_dynamic-slice_fusion
  117.4 1.9 constant_dynamic-slice_fusion.1
  120.0 1.8 maximum_add_fusion
  121.9 1.8 copy-done.2
  123.8 1.6 collective-permute-start.3
  125.3 12.1 %collective-permute-done.3 = bf16[1216,384]{1,0:T(8,128)(2,1)S(1)} collective-permute-done((bf16[1216,384]{1,0:T(8,128)(2,1)S(1)}, bf16[1216,384]{1,0:T(8,128)(2,1)S(1)}, u32[]{:S(2)}, u32[]{:S(2)}) %collective-permute-start.3) | collective-permute-done | bytes 933920 | tf_op jit(solution)/shard_map/ppermute | solution.py:425
  137.4 1.7 convert_add_fusion
  139.3 8.5 %collective-permute-done.4 = bf16[608,384]{1,0:T(8,128)(2,1)S(1)} collective-permute-done((bf16[608,384]{1,0:T(8,128)(2,1)S(1)}, bf16[608,384]{1,0:T(8,128)(2,1)S(1)}, u32[]{:S(2)}, u32[]{:S(2)}) %collective-permute-start.4) | collective-permute-done | bytes 466976 | tf_op jit(solution)/shard_map/ppermute | solution.py:425
  148.0 6.0 %collective-permute-done.5 = bf16[304,384]{1,0:T(8,128)(2,1)S(1)} collective-permute-done((bf16[304,384]{1,0:T(8,128)(2,1)S(1)}, bf16[304,384]{1,0:T(8,128)(2,1)S(1)}, u32[]{:S(2)}, u32[]{:S(2)}) %collective-permute-start.5) | collective-permute-done | bytes 233504 | tf_op jit(solution)/shard_map/ppermute | solution.py:425
  154.7 7.5 %collective-permute-done.6 = bf16[152,384]{1,0:T(8,128)(2,1)S(1)} collective-permute-done((bf16[152,384]{1,0:T(8,128)(2,1)S(1)}, bf16[152,384]{1,0:T(8,128)(2,1)S(1)}, u32[]{:S(2)}, u32[]{:S(2)}) %collective-permute-start.6) | collective-permute-done | bytes 116768 | tf_op jit(solution)/shard_map/ppermute | solution.py:425
  162.3 6.2 %collective-permute-done.7 = bf16[152,384]{1,0:T(8,128)(2,1)S(1)} collective-permute-done((bf16[152,384]{1,0:T(8,128)(2,1)S(1)}, bf16[152,384]{1,0:T(8,128)(2,1)S(1)}, u32[]{:S(2)}, u32[]{:S(2)}) %collective-permute-start.7) | collective-permute-done | bytes 116768 | tf_op jit(solution)/shard_map/ppermute | solution.py:425
  168.6 6.0 %collective-permute-done.8 = bf16[304,384]{1,0:T(8,128)(2,1)S(1)} collective-permute-done((bf16[304,384]{1,0:T(8,128)(2,1)S(1)}, bf16[304,384]{1,0:T(8,128)(2,1)S(1)}, u32[]{:S(2)}, u32[]{:S(2)}) %collective-permute-start.8) | collective-permute-done | bytes 233504 | tf_op jit(solution)/shard_map/ppermute | solution.py:425
  174.9 8.5 %collective-permute-done.9 = bf16[608,384]{1,0:T(8,128)(2,1)S(1)} collective-permute-done((bf16[608,384]{1,0:T(8,128)(2,1)S(1)}, bf16[608,384]{1,0:T(8,128)(2,1)S(1)}, u32[]{:S(2)}, u32[]{:S(2)}) %collective-permute-start.9) | collective-permute-done | bytes 466976 | tf_op jit(solution)/shard_map/ppermute | solution.py:425
  183.8 1.6 collective-permute-start.10
  185.4 12.2 %collective-permute-done.10 = bf16[1216,384]{1,0:T(8,128)(2,1)} collective-permute-done((bf16[1216,384]{1,0:T(8,128)(2,1)S(1)}, bf16[1216,384]{1,0:T(8,128)(2,1)}, u32[]{:S(2)}, u32[]{:S(2)}) %collective-permute-start.10) | collective-permute-done | bytes 933920 | tf_op jit(solution)/shard_map/ppermute | solution.py:425
  197.5 2.1 maximum_select_fusion.1
  199.8 16.8 %collective-permute-done.1 = bf16[4,168,384]{2,1,0:T(8,128)(2,1)S(1)} collective-permute-done((bf16[4,168,384]{2,1,0:T(8,128)(2,1)S(1)}, bf16[4,168,384]{2,1,0:T(8,128)(2,1)S(1)}, u32[]{:S(2)}, u32[]{:S(2)}) %collective-permute-start.1) | collective-permute-done | bytes 516128 | tf_op jit(solution)/shard_map/ppermute | solution.py:640
  216.6 2.9 %pad_maximum_fusion = f32[4,392,384]{2,1,0:T(8,128)} fusion(f32[4,224,384]{2,1,0:T(8,128)} %get-tuple-element.32, f32[4,168,384]{2,1,0:T(8,128)S(1)} %convert_element_type.80), kind=kLoop, calls=%fused_computation.5 | loop fusion | flops 602112 | bytes 4816896 | tf_op jit(solution)/shard_map/concatenate | solution.py:641
  219.8 1.5 slice.120
  222.8 1.6 slice.130
  226.0 1.6 fusion.41
  229.8 1.5 slice_reduce_fusion.5
  231.3 1.7 reshape.455
  234.6 1.8 reshape.456
  236.4 1.9 fusion.1
  238.9 2.4 pad_maximum_fusion.3
  241.3 1.7 pad_maximum_fusion.1
  (115 shorter events, 25.2 us)
Async XLA Ops:
  0.6 10.2 %copy-start = (bf16[169,12]{0,1:T(8,128)(2,1)S(1)}, bf16[169,12]{0,1:T(8,128)(2,1)}, u32[]{:S(2)}) copy-start(bf16[169,12]{0,1:T(8,128)(2,1)} %param.24) | copy-start | bytes 12172
  1.8 18.9 %collective-permute-start = (bf16[4,168,384]{2,1,0:T(8,128)(2,1)S(1)}, bf16[4,168,384]{2,1,0:T(8,128)(2,1)S(1)}, u32[]{:S(2)}, u32[]{:S(2)}) collective-permute-start(bf16[4,168,384]{2,1,0:T(8,128)(2,1)S(1)} %bitcast.28), channel_id=1, source_target_pairs={{0,28},{4,0},{8,4},{12,8},{16,12},{20,16},{24,20},{28,24},{1,29},{... | collective-permute-start | bytes 1548296 | tf_op jit(solution)/shard_map/ppermute | solution.py:500
  10.3 0.6 copy-start.4
  11.6 0.8 copy-start.6
  12.1 4.1 %copy-start.8 = (bf16[384]{0:T(512)(128)(2,1)S(1)}, bf16[384]{0:T(512)(128)(2,1)}, u32[]{:S(2)}) copy-start(bf16[384]{0:T(512)(128)(2,1)} %param.20) | copy-start | bytes 2308
  12.1 4.1 %copy-start.9 = (bf16[384]{0:T(512)(128)(2,1)S(1)}, bf16[384]{0:T(512)(128)(2,1)}, u32[]{:S(2)}) copy-start(bf16[384]{0:T(512)(128)(2,1)} %param.21) | copy-start | bytes 2308
  12.1 4.1 %copy-start.10 = (bf16[384]{0:T(512)(128)(2,1)S(1)}, bf16[384]{0:T(512)(128)(2,1)}, u32[]{:S(2)}) copy-start(bf16[384]{0:T(512)(128)(2,1)} %param.26) | copy-start | bytes 2308
  12.1 4.1 %copy-start.11 = (bf16[384]{0:T(512)(128)(2,1)S(1)}, bf16[384]{0:T(512)(128)(2,1)}, u32[]{:S(2)}) copy-start(bf16[384]{0:T(512)(128)(2,1)} %param.27) | copy-start | bytes 2308
  12.1 4.1 %copy-start.12 = (bf16[384]{0:T(512)(128)(2,1)S(1)}, bf16[384]{0:T(512)(128)(2,1)}, u32[]{:S(2)}) copy-start(bf16[384]{0:T(512)(128)(2,1)} %param.28) | copy-start | bytes 2308
  12.1 4.1 %copy-start.13 = (bf16[384]{0:T(512)(128)(2,1)S(1)}, bf16[384]{0:T(512)(128)(2,1)}, u32[]{:S(2)}) copy-start(bf16[384]{0:T(512)(128)(2,1)} %param.32) | copy-start | bytes 2308
  12.2 4.1 %copy-start.5 = (bf16[1536]{0:T(1024)(128)(2,1)S(1)}, bf16[1536]{0:T(1024)(128)(2,1)}, u32[]{:S(2)}) copy-start(bf16[1536]{0:T(1024)(128)(2,1)} %param.30) | copy-start | bytes 9220
  12.2 4.7 %copy-start.7 = (s32[4,2]{0,1:T(2,128)S(1)}, s32[4,2]{0,1:T(2,128)}, u32[]{:S(2)}) copy-start(s32[4,2]{0,1:T(2,128)} %param.19) | copy-start | bytes 100
  20.6 0.8 copy-start.3
  116.0 4.0 %collective-permute-start.2 = (bf16[2432,384]{1,0:T(8,128)(2,1)S(1)}, bf16[2432,384]{1,0:T(8,128)(2,1)}, u32[]{:S(2)}, u32[]{:S(2)}) collective-permute-start(bf16[2432,384]{1,0:T(8,128)(2,1)S(1)} %pad_maximum_fusion.2), channel_id=1, source_target_pairs={{0,1},{1,0},{2,3},{3,2},{4,5},{5,4},{6,7},{7,6},{8,9},{9,8},{10,11... | collective-permute-start | bytes 5603336 | tf_op jit(solution)/shard_map/ppermute | solution.py:425
  121.8 1.8 copy-start.2
  123.8 13.6 %collective-permute-start.3 = (bf16[1216,384]{1,0:T(8,128)(2,1)S(1)}, bf16[1216,384]{1,0:T(8,128)(2,1)S(1)}, u32[]{:S(2)}, u32[]{:S(2)}) collective-permute-start(bf16[1216,384]{1,0:T(8,128)(2,1)S(1)} %dynamic-slice_convert_fusion.1), channel_id=1, source_target_pairs={{0,2},{1,9},{2,0},{3,11},{4,6},{5,13},{6,4},{7,15},{8,10},{9,1},{1... | collective-permute-start | bytes 2801672 | tf_op jit(solution)/shard_map/ppermute | solution.py:425
  139.2 8.6 %collective-permute-start.4 = (bf16[608,384]{1,0:T(8,128)(2,1)S(1)}, bf16[608,384]{1,0:T(8,128)(2,1)S(1)}, u32[]{:S(2)}, u32[]{:S(2)}) collective-permute-start(bf16[608,384]{1,0:T(8,128)(2,1)S(1)} %dynamic-slice_convert_fusion.3), channel_id=1, source_target_pairs={{0,4},{1,3},{2,6},{3,1},{4,0},{5,7},{6,2},{7,5},{8,12},{9,11},{10,... | collective-permute-start | bytes 1400840 | tf_op jit(solution)/shard_map/ppermute | solution.py:425
  147.9 6.1 %collective-permute-start.5 = (bf16[304,384]{1,0:T(8,128)(2,1)S(1)}, bf16[304,384]{1,0:T(8,128)(2,1)S(1)}, u32[]{:S(2)}, u32[]{:S(2)}) collective-permute-start(bf16[304,384]{1,0:T(8,128)(2,1)S(1)} %dynamic-slice_convert_fusion.4), channel_id=1, source_target_pairs={{0,8},{1,5},{2,10},{3,7},{4,12},{5,1},{6,14},{7,3},{8,0},{9,13},{1... | collective-permute-start | bytes 700424 | tf_op jit(solution)/shard_map/ppermute | solution.py:425
  154.2 8.0 %collective-permute-start.6 = (bf16[152,384]{1,0:T(8,128)(2,1)S(1)}, bf16[152,384]{1,0:T(8,128)(2,1)S(1)}, u32[]{:S(2)}, u32[]{:S(2)}) collective-permute-start(bf16[152,384]{1,0:T(8,128)(2,1)S(1)} %dynamic-slice_convert_fusion.5), channel_id=1, source_target_pairs={{0,16},{1,17},{2,18},{3,19},{4,20},{5,21},{6,22},{7,23},{8,24},{9,... | collective-permute-start | bytes 350216 | tf_op jit(solution)/shard_map/ppermute | solution.py:425
  162.2 6.3 %collective-permute-start.7 = (bf16[152,384]{1,0:T(8,128)(2,1)S(1)}, bf16[152,384]{1,0:T(8,128)(2,1)S(1)}, u32[]{:S(2)}, u32[]{:S(2)}) collective-permute-start(bf16[152,384]{1,0:T(8,128)(2,1)S(1)} %add_convert_fusion), channel_id=1, source_target_pairs={{0,16},{1,17},{2,18},{3,19},{4,20},{5,21},{6,22},{7,23},{8,24},{9,... | collective-permute-start | bytes 350216 | tf_op jit(solution)/shard_map/ppermute | solution.py:425
  168.5 6.1 %collective-permute-start.8 = (bf16[304,384]{1,0:T(8,128)(2,1)S(1)}, bf16[304,384]{1,0:T(8,128)(2,1)S(1)}, u32[]{:S(2)}, u32[]{:S(2)}) collective-permute-start(bf16[304,384]{1,0:T(8,128)(2,1)S(1)} %maximum_select_fusion.5), channel_id=1, source_target_pairs={{0,8},{1,5},{2,10},{3,7},{4,12},{5,1},{6,14},{7,3},{8,0},{9,13},{1... | collective-permute-start | bytes 700424 | tf_op jit(solution)/shard_map/ppermute | solution.py:425
  174.8 8.6 %collective-permute-start.9 = (bf16[608,384]{1,0:T(8,128)(2,1)S(1)}, bf16[608,384]{1,0:T(8,128)(2,1)S(1)}, u32[]{:S(2)}, u32[]{:S(2)}) collective-permute-start(bf16[608,384]{1,0:T(8,128)(2,1)S(1)} %maximum_select_fusion.4), channel_id=1, source_target_pairs={{0,4},{1,3},{2,6},{3,1},{4,0},{5,7},{6,2},{7,5},{8,12},{9,11},{10,... | collective-permute-start | bytes 1400840 | tf_op jit(solution)/shard_map/ppermute | solution.py:425
  183.8 15.9 %copy-start.14 = (bf16[4,168,384]{2,1,0:T(8,128)(2,1)S(1)}, bf16[4,168,384]{2,1,0:T(8,128)(2,1)}, u32[]{:S(2)}) copy-start(bf16[4,168,384]{2,1,0:T(8,128)(2,1)} %get-tuple-element.31) | copy-start | bytes 1548292
  183.8 13.7 %collective-permute-start.10 = (bf16[1216,384]{1,0:T(8,128)(2,1)S(1)}, bf16[1216,384]{1,0:T(8,128)(2,1)}, u32[]{:S(2)}, u32[]{:S(2)}) collective-permute-start(bf16[1216,384]{1,0:T(8,128)(2,1)S(1)} %maximum_select_fusion.3), channel_id=1, source_target_pairs={{0,2},{1,9},{2,0},{3,11},{4,6},{5,13},{6,4},{7,15},{8,10},{9,1},{1... | collective-permute-start | bytes 2801672 | tf_op jit(solution)/shard_map/ppermute | solution.py:425
  199.6 20.1 %collective-permute-start.11 = (bf16[2432,384]{1,0:T(8,128)(2,1)S(1)}, bf16[2432,384]{1,0:T(8,128)(2,1)}, u32[]{:S(2)}, u32[]{:S(2)}) collective-permute-start(bf16[2432,384]{1,0:T(8,128)(2,1)S(1)} %maximum_select_fusion.1), channel_id=1, source_target_pairs={{0,1},{1,0},{2,3},{3,2},{4,5},{5,4},{6,7},{7,6},{8,9},{9,8},{10,11... | collective-permute-start | bytes 5603336 | tf_op jit(solution)/shard_map/ppermute | solution.py:425
  199.7 16.8 %collective-permute-start.1 = (bf16[4,168,384]{2,1,0:T(8,128)(2,1)S(1)}, bf16[4,168,384]{2,1,0:T(8,128)(2,1)S(1)}, u32[]{:S(2)}, u32[]{:S(2)}) collective-permute-start(bf16[4,168,384]{2,1,0:T(8,128)(2,1)S(1)} %copy-done.14), channel_id=1, source_target_pairs={{0,4},{4,8},{8,12},{12,16},{16,20},{20,24},{24,28},{28,0},{1,5},{5... | collective-permute-start | bytes 1548296 | tf_op jit(solution)/shard_map/ppermute | solution.py:640
  241.3 1.7 copy-start.1
